TPU v7x, 256 devices: a whole 4x4x8 slice. The times are simulated.
256 devices in a mesh: chan: 32 (over x_hi, z, core), bfly: 2 (over x_lo), samp: 4 (over y).
Axes of the slice: x: 4 (x_hi: 2, x_lo: 2; x = x_hi * 2 + x_lo), y: 4, z: 8, core: 2. Of those that a mesh axis runs over, the one named last changes fastest.
Arguments:
- features: bfloat16 [65536, 2048], P(('chan', 'bfly'), 'samp'), may hold values from -6 to 6
- cotangent: bfloat16 [65536, 2048], P(('chan', 'bfly'), 'samp'), may hold values from -6 to 6
- right_factor: bfloat16 [2, 256, 256, 256], P(None, ('chan', 'bfly')), may hold values from -0.375 to 0.375
- left_factor: float32 [2, 256, 256, 256], P(None, ('chan', 'bfly')), may hold values from -0.375 to 0.375
- mixing: float32 [2, 2, 256, 256], P(None, None, ('chan', 'bfly')), may hold values from -1.2 to 1.2
Outputs:
- output: bfloat16 [65536, 2048], P(('chan', 'bfly'), 'samp')
- feature_grad: bfloat16 [65536, 2048], P(('chan', 'bfly'), 'samp')
- grad_right: float32 [2, 256, 256, 256], P(None, ('chan', 'bfly'))
- grad_left: float32 [2, 256, 256, 256], P(None, ('chan', 'bfly'))
- grad_mixing: float32 [2, 2, 256, 256], P(None, None, ('chan', 'bfly'))
All inputs are finite; a program needn't handle non-finite values.
Results may differ from a plain program's by a relative error of at most 0.025.
Values may be sent and summed in bfloat16 or wider, within the bound.
A program may use at most 128 MiB of HBM per device.

v0:
```python
import jax
import jax.numpy as jnp
from jax import lax
from jax.sharding import PartitionSpec as P

BLOCK = 256
LAYERS = 2


def partner_2(block, axis, distance):
    count = lax.axis_size(axis)
    route = []
    for low in range(count):
        high = low | 1 << distance
        if high != low and high < count:
            route += [(low, high), (high, low)]
    return lax.ppermute(block, axis, route)


def to_columns(values):
    return lax.all_to_all(values, ("chan", "bfly"), split_axis=1, concat_axis=0, tiled=True)


def to_rows(values):
    return lax.all_to_all(values, ("chan", "bfly"), split_axis=0, concat_axis=1, tiled=True)


def local(features, cotangent, right_factor, left_factor, mixing):
    blocks = right_factor.shape[1]
    samples = features.shape[1]
    height = features.reshape(blocks, BLOCK, samples)
    saved = []
    for layer_index in range(LAYERS):
        mixed_u = jnp.einsum(
            "bis,bij->bjs", height, right_factor[layer_index], preferred_element_type=jnp.float32
        ).astype(jnp.bfloat16)
        self_gain = mixing[layer_index, 0][:, :, None]
        cross_gain = mixing[layer_index, 1][:, :, None]
        partner = partner_2(mixed_u, "bfly", 0)
        mixed_v = (self_gain * mixed_u + cross_gain * partner).astype(jnp.bfloat16)
        columns = to_columns(mixed_v)
        kept = (mixed_u, partner)
        outer = jnp.einsum(
            "bjs,jbk->kjs", columns, left_factor[layer_index], preferred_element_type=jnp.float32
        ).astype(jnp.bfloat16)
        activation = to_rows(outer)
        saved.append((height, kept, columns, activation))
        height = (height.astype(jnp.float32) + jax.nn.silu(activation.astype(jnp.float32))).astype(
            jnp.bfloat16
        )
    output = height.reshape(blocks * BLOCK, samples)
    grad = cotangent.reshape(blocks, BLOCK, samples)
    rights = [None] * LAYERS
    lefts = [None] * LAYERS
    mixes = [None] * LAYERS
    for layer_index in reversed(range(LAYERS)):
        height_in, kept, columns, activation = saved[layer_index]
        before = activation.astype(jnp.float32)
        logistic = jax.nn.sigmoid(before)
        error = (grad.astype(jnp.float32) * logistic * (1.0 + before * (1.0 - logistic))).astype(
            jnp.bfloat16
        )
        error_cols = to_columns(error)
        grad_left = jnp.einsum(
            "bjs,kjs->jbk", columns, error_cols, preferred_element_type=jnp.float32
        )
        grad_cols = jnp.einsum(
            "jbk,kjs->bjs", left_factor[layer_index], error_cols, preferred_element_type=jnp.float32
        ).astype(jnp.bfloat16)
        mixed_u, partner = kept
        self_gain = mixing[layer_index, 0][:, :, None]
        cross_gain = mixing[layer_index, 1][:, :, None]
        grad_v = to_rows(grad_cols)
        grad_mix = jnp.stack(
            [
                jnp.einsum("bjs,bjs->bj", grad_v, mixed_u, preferred_element_type=jnp.float32),
                jnp.einsum("bjs,bjs->bj", grad_v, partner, preferred_element_type=jnp.float32),
            ]
        )
        carried = (cross_gain * grad_v).astype(jnp.bfloat16)
        returned = partner_2(carried, "bfly", 0)
        grad_u = (self_gain * grad_v + returned.astype(jnp.float32)).astype(jnp.bfloat16)
        grad_right = jnp.einsum(
            "bis,bjs->bij", height_in, grad_u, preferred_element_type=jnp.float32
        )
        back_term = jnp.einsum(
            "bij,bjs->bis", right_factor[layer_index], grad_u, preferred_element_type=jnp.float32
        )
        grad = (grad.astype(jnp.float32) + back_term).astype(jnp.bfloat16)
        rights[layer_index] = grad_right
        lefts[layer_index] = grad_left
        mixes[layer_index] = grad_mix
    all_right = jnp.stack(rights)
    all_left = jnp.stack(lefts)
    all_mix = jnp.stack(mixes)
    all_right, all_left, all_mix = (
        lax.psum(all_right.astype(jnp.bfloat16), "samp").astype(jnp.float32),
        lax.psum(all_left.astype(jnp.bfloat16), "samp").astype(jnp.float32),
        lax.psum(all_mix.astype(jnp.bfloat16), "samp").astype(jnp.float32),
    )
    return (output, grad.reshape(blocks * BLOCK, samples), all_right, all_left, all_mix)


def solution(mesh):
    in_specs = (
        P(("chan", "bfly"), "samp"),
        P(("chan", "bfly"), "samp"),
        P(None, ("chan", "bfly"), None, None),
        P(None, ("chan", "bfly"), None, None),
        P(None, None, ("chan", "bfly"), None),
    )
    out_specs = (
        P(("chan", "bfly"), "samp"),
        P(("chan", "bfly"), "samp"),
        P(None, ("chan", "bfly"), None, None),
        P(None, ("chan", "bfly"), None, None),
        P(None, None, ("chan", "bfly"), None),
    )
    return jax.shard_map(local, mesh=mesh, in_specs=in_specs, out_specs=out_specs, check_vma=False)
```

profile of v0, /device:TPU:1, one launch (start us, length us, event | category | flops | bytes accessed | tf_op | source)
XLA Modules:
  0.0 527.4 jit_solution(5031912849368408522)
XLA Ops:
  9.1 2.1 collective-permute-start
  11.2 21.5 %collective-permute-done = bf16[4,256,512]{2,1,0:T(8,128)(2,1)S(1)} collective-permute-done((bf16[4,256,512]{2,1,0:T(8,128)(2,1)S(1)}, bf16[4,256,512]{2,1,0:T(8,128)(2,1)S(1)}, u32[]{:S(2)}, u32[]{:S(2)}) %collective-permute-start) | collective-permute-done | bytes 1048608 | tf_op jit(solution)/shard_map/ppermute | solution.py:17
  34.7 43.4 %all_to_all.126 = bf16[4,256,512]{2,0,1:T(4,128)(2,1)S(1)} all-to-all(bf16[4,256,512]{2,0,1:T(4,128)(2,1)S(1)} %copy.92), channel_id=1, replica_groups=mesh['chan'=32,'bfly'=2,'samp'=4] {'chan','bfly'}, dimensions={1} | all-to-all | bytes 2097152 | tf_op jit(solution)/shard_map/all_to_all | solution.py:21
  82.0 34.5 %all_to_all.127 = bf16[256,4,512]{2,1,0:T(4,128)(2,1)S(1)} all-to-all(bf16[256,4,512]{2,1,0:T(4,128)(2,1)S(1)} %copy.95), channel_id=1, replica_groups=mesh['chan'=32,'bfly'=2,'samp'=4] {'chan','bfly'}, dimensions={0} | all-to-all | bytes 2097152 | tf_op jit(solution)/shard_map/all_to_all | solution.py:25
  119.0 2.4 add_convert_fusion.1
  123.7 22.6 %collective-permute-done.1 = bf16[4,256,512]{1,2,0:T(8,128)(2,1)S(1)} collective-permute-done((bf16[4,256,512]{1,2,0:T(8,128)(2,1)S(1)}, bf16[4,256,512]{1,2,0:T(8,128)(2,1)S(1)}, u32[]{:S(2)}, u32[]{:S(2)}) %collective-permute-start.1) | collective-permute-done | bytes 1048608 | tf_op jit(solution)/shard_map/ppermute | solution.py:17
  148.7 2.6 copy.99
  151.3 35.6 %all_to_all.128 = bf16[4,256,512]{2,0,1:T(4,128)(2,1)S(1)} all-to-all(bf16[4,256,512]{2,0,1:T(4,128)(2,1)} %copy.99), channel_id=1, replica_groups=mesh['chan'=32,'bfly'=2,'samp'=4] {'chan','bfly'}, dimensions={1} | all-to-all | bytes 2097152 | tf_op jit(solution)/shard_map/all_to_all | solution.py:21
  190.0 2.6 copy.102
  192.6 34.7 %all_to_all.129 = bf16[256,4,512]{2,1,0:T(4,128)(2,1)S(1)} all-to-all(bf16[256,4,512]{2,1,0:T(4,128)(2,1)} %copy.102), channel_id=1, replica_groups=mesh['chan'=32,'bfly'=2,'samp'=4] {'chan','bfly'}, dimensions={0} | all-to-all | bytes 2097152 | tf_op jit(solution)/shard_map/all_to_all | solution.py:25
  229.3 2.9 reshape.48
  232.3 2.7 fusion.13
  235.8 34.6 %all_to_all.130 = bf16[4,256,512]{2,0,1:T(4,128)(2,1)S(1)} all-to-all(bf16[4,256,512]{2,0,1:T(4,128)(2,1)S(1)} %copy.105), channel_id=1, replica_groups=mesh['chan'=32,'bfly'=2,'samp'=4] {'chan','bfly'}, dimensions={1} | all-to-all | bytes 2097152 | tf_op jit(solution)/shard_map/all_to_all | solution.py:21
  273.5 2.6 copy.108
  276.1 34.7 %all_to_all.131 = bf16[256,4,512]{2,1,0:T(4,128)(2,1)S(1)} all-to-all(bf16[256,4,512]{2,1,0:T(4,128)(2,1)} %copy.108), channel_id=1, replica_groups=mesh['chan'=32,'bfly'=2,'samp'=4] {'chan','bfly'}, dimensions={0} | all-to-all | bytes 2097152 | tf_op jit(solution)/shard_map/all_to_all | solution.py:25
  312.3 2.4 copy.110
  318.2 22.6 %collective-permute-done.2 = bf16[4,256,512]{1,2,0:T(8,128)(2,1)S(1)} collective-permute-done((bf16[4,256,512]{1,2,0:T(8,128)(2,1)S(1)}, bf16[4,256,512]{1,2,0:T(8,128)(2,1)S(1)}, u32[]{:S(2)}, u32[]{:S(2)}) %collective-permute-start.2) | collective-permute-done | bytes 1048608 | tf_op jit(solution)/shard_map/ppermute | solution.py:17
  340.9 4.4 fusion.10
  346.1 35.4 %all_to_all.132 = bf16[4,256,512]{2,0,1:T(4,128)(2,1)S(1)} all-to-all(bf16[4,256,512]{2,0,1:T(4,128)(2,1)S(1)} %copy.112), channel_id=1, replica_groups=mesh['chan'=32,'bfly'=2,'samp'=4] {'chan','bfly'}, dimensions={1} | all-to-all | bytes 2097152 | tf_op jit(solution)/shard_map/all_to_all | solution.py:21
  384.5 2.6 copy.115
  387.1 34.7 %all_to_all.133 = bf16[256,4,512]{2,1,0:T(4,128)(2,1)S(1)} all-to-all(bf16[256,4,512]{2,1,0:T(4,128)(2,1)} %copy.115), channel_id=1, replica_groups=mesh['chan'=32,'bfly'=2,'samp'=4] {'chan','bfly'}, dimensions={0} | all-to-all | bytes 2097152 | tf_op jit(solution)/shard_map/all_to_all | solution.py:25
  423.1 2.1 all_to_all.117
  425.3 2.8 fusion.18
  433.8 19.0 %collective-permute-done.3 = bf16[4,256,512]{2,1,0:T(8,128)(2,1)S(1)} collective-permute-done((bf16[4,256,512]{2,1,0:T(8,128)(2,1)S(1)}, bf16[4,256,512]{2,1,0:T(8,128)(2,1)S(1)}, u32[]{:S(2)}, u32[]{:S(2)}) %collective-permute-start.3) | collective-permute-done | bytes 1048608 | tf_op jit(solution)/shard_map/ppermute | solution.py:17
  456.7 3.0 reshape.46
  459.7 4.5 add_convert_fusion
  465.9 3.0 copy.141
  468.9 2.1 fusion.4
  471.0 10.0 %psum.23 = bf16[2,2,4,256]{3,2,1,0:T(4,128)(2,1)S(1)} all-reduce(bf16[2,2,4,256]{3,2,1,0:T(4,128)(2,1)S(1)} %pad_maximum_fusion.2), channel_id=1, replica_groups=mesh['chan'=32,'bfly'=2,'samp'=4] {'samp'}, use_global_device_ids=true, to_apply=%region_2.3 | all-reduce | flops 4096 | bytes 16384 | tf_op jit(solution)/shard_map/psum | solution.py:99
  481.7 3.4 fusion.11
  485.0 31.4 %all-reduce.3.cloned.1.call-done = (bf16[2,4,256,256]{2,3,1,0:T(8,128)(2,1)}, bf16[2,4,256,256]{3,2,1,0:T(8,128)(2,1)}) async-done(((bf16[2,4,256,256]{2,3,1,0:T(8,128)(2,1)}, bf16[2,4,256,256]{3,2,1,0:T(8,128)(2,1)}), (bf16[2,4,256,256]{2,3,1,0:T(8,128)(2,1)}, bf16[2,4,256,256]{3,2,1,0:T(8,128)(2,1)})) %all-reduce.3.cloned.1.call-update) | async-done | bytes 2097168 | tf_op jit(solution)/shard_map/psum | solution.py:97
  516.4 2.7 copy.124
  (108 shorter events, 47.3 us)
Async XLA Ops:
  7.2 4.1 copy-start.32
  7.2 509.2 %all-reduce.3.cloned.1.call-start = ((), (), s32[]{:S(2)}) async-start(), calls=%async_computation.8 | async-start | bytes 4194304 | tf_op jit(solution)/shard_map/psum | solution.py:97
  9.1 25.5 %copy-start.1 = (bf16[4,256,512]{2,1,0:T(8,128)(2,1)}, bf16[4,256,512]{2,1,0:T(8,128)(2,1)S(1)}, u32[]{:S(2)}) copy-start(bf16[4,256,512]{2,1,0:T(8,128)(2,1)S(1)} %convolution_convert_fusion.5) | copy-start | bytes 3145732
  9.1 23.7 %collective-permute-start = (bf16[4,256,512]{2,1,0:T(8,128)(2,1)S(1)}, bf16[4,256,512]{2,1,0:T(8,128)(2,1)S(1)}, u32[]{:S(2)}, u32[]{:S(2)}) collective-permute-start(bf16[4,256,512]{2,1,0:T(8,128)(2,1)S(1)} %convolution_convert_fusion.5), channel_id=1, source_target_pairs={{0,4},{4,0},{1,5},{5,1},{2,6},{6,2},{3,7},{7,3},{8,12},{12,8},{9,1... | collective-permute-start | bytes 3145736 | tf_op jit(solution)/shard_map/ppermute | solution.py:17
  34.7 44.0 %copy-start.11 = (f32[2,4,256,256]{3,2,1,0:T(8,128)S(1)}, f32[2,4,256,256]{3,2,1,0:T(8,128)}, u32[]{:S(2)}) copy-start(f32[2,4,256,256]{3,2,1,0:T(8,128)} %param.8) | copy-start | bytes 6291460
  78.6 3.4 copy-start.17
  117.2 1.7 copy-start.4
  119.0 2.4 copy-start.26
  121.4 24.9 %copy-start.7 = (bf16[4,256,512]{2,1,0:T(8,128)(2,1)}, bf16[4,256,512]{2,1,0:T(8,128)(2,1)S(1)}, u32[]{:S(2)}) copy-start(bf16[4,256,512]{2,1,0:T(8,128)(2,1)S(1)} %add_convert_fusion.1) | copy-start | bytes 3145732
  121.9 24.4 %collective-permute-start.1 = (bf16[4,256,512]{1,2,0:T(8,128)(2,1)S(1)}, bf16[4,256,512]{1,2,0:T(8,128)(2,1)S(1)}, u32[]{:S(2)}, u32[]{:S(2)}) collective-permute-start(bf16[4,256,512]{1,2,0:T(8,128)(2,1)S(1)} %fusion.24), channel_id=1, source_target_pairs={{0,4},{4,0},{1,5},{5,1},{2,6},{6,2},{3,7},{7,3},{8,12},{12,8},{9,1... | collective-permute-start | bytes 3145736 | tf_op jit(solution)/shard_map/ppermute | solution.py:17
  151.3 37.1 %copy-start.12 = (f32[2,4,256,256]{3,2,1,0:T(8,128)S(1)}, f32[2,4,256,256]{3,2,1,0:T(8,128)}, u32[]{:S(2)}) copy-start(f32[2,4,256,256]{3,2,1,0:T(8,128)} %param.8) | copy-start | bytes 6291460
  235.8 36.1 %copy-start.13 = (f32[2,4,256,256]{3,2,1,0:T(8,128)S(1)}, f32[2,4,256,256]{3,2,1,0:T(8,128)}, u32[]{:S(2)}) copy-start(f32[2,4,256,256]{3,2,1,0:T(8,128)} %param.8) | copy-start | bytes 6291460
  314.7 26.2 %copy-start.2 = (bf16[4,256,512]{1,2,0:T(8,128)(2,1)S(1)}, bf16[4,256,512]{1,2,0:T(8,128)(2,1)}, u32[]{:S(2)}) copy-start(bf16[4,256,512]{1,2,0:T(8,128)(2,1)} %copy.110) | copy-start | bytes 3145732
  314.7 26.2 %copy-start.27 = (bf16[2,4,256,256]{3,2,1,0:T(8,128)(2,1)S(1)}, bf16[2,4,256,256]{3,2,1,0:T(8,128)(2,1)}, u32[]{:S(2)}) copy-start(bf16[2,4,256,256]{3,2,1,0:T(8,128)(2,1)} %param.7) | copy-start | bytes 3145732
  316.2 24.6 %collective-permute-start.2 = (bf16[4,256,512]{1,2,0:T(8,128)(2,1)S(1)}, bf16[4,256,512]{1,2,0:T(8,128)(2,1)S(1)}, u32[]{:S(2)}, u32[]{:S(2)}) collective-permute-start(bf16[4,256,512]{1,2,0:T(8,128)(2,1)S(1)} %fusion.8), channel_id=1, source_target_pairs={{0,4},{4,0},{1,5},{5,1},{2,6},{6,2},{3,7},{7,3},{8,12},{12,8},{9,1... | collective-permute-start | bytes 3145736 | tf_op jit(solution)/shard_map/ppermute | solution.py:17
  340.9 4.4 copy-start.30
  346.1 36.9 %copy-start.14 = (f32[2,4,256,256]{3,2,1,0:T(8,128)S(1)}, f32[2,4,256,256]{3,2,1,0:T(8,128)}, u32[]{:S(2)}) copy-start(f32[2,4,256,256]{3,2,1,0:T(8,128)} %param.8) | copy-start | bytes 6291460
  425.3 4.9 copy-start.20
  425.3 4.9 copy-start.22
  428.1 2.5 copy-start.3
  428.1 2.5 copy-start.8
  428.1 2.5 copy-start.31
  428.1 24.7 %collective-permute-start.3 = (bf16[4,256,512]{2,1,0:T(8,128)(2,1)S(1)}, bf16[4,256,512]{2,1,0:T(8,128)(2,1)S(1)}, u32[]{:S(2)}, u32[]{:S(2)}) collective-permute-start(bf16[4,256,512]{2,1,0:T(8,128)(2,1)S(1)} %get-tuple-element.31), channel_id=1, source_target_pairs={{0,4},{4,0},{1,5},{5,1},{2,6},{6,2},{3,7},{7,3},{8,12},{12,8},{9,1... | collective-permute-start | bytes 3145736 | tf_op jit(solution)/shard_map/ppermute | solution.py:17
  430.7 1.2 copy-start.18
  430.7 1.5 copy-start.24
  432.2 20.6 %copy-start.5 = (bf16[1024,512]{1,0:T(8,128)(2,1)S(1)}, bf16[1024,512]{1,0:T(8,128)(2,1)}, u32[]{:S(2)}) copy-start(bf16[1024,512]{1,0:T(8,128)(2,1)} %param.5) | copy-start | bytes 3145732
  432.2 20.6 %copy-start.9 = (bf16[4,256,512]{2,1,0:T(8,128)(2,1)S(1)}, bf16[4,256,512]{2,1,0:T(8,128)(2,1)}, u32[]{:S(2)}) copy-start(bf16[4,256,512]{2,1,0:T(8,128)(2,1)} %all_to_all.117) | copy-start | bytes 3145732
  456.7 3.0 copy-start.6
  459.7 4.5 copy-start
  465.9 3.0 copy-start.16
  468.9 12.8 %copy-start.10 = (bf16[4,256,512]{2,1,0:T(8,128)(2,1)S(1)}, bf16[4,256,512]{2,1,0:T(8,128)(2,1)}, u32[]{:S(2)}) copy-start(bf16[4,256,512]{2,1,0:T(8,128)(2,1)} %all_to_all.117) | copy-start | bytes 3145732
  516.4 2.7 copy-start.28
  (6 other events, 6.0 us)
Sparse Core Ops, SparseCore 0:
  455.1 61.3 all-reduce.2
where the time goes:
time: 528 us; the launch traced here: 527 us
  blocking collectives  297 us (56%)
  waiting for transfers between devices  117 us (22%)
  local copies, waits for them, and re-layouts  47.4 us (9%)
  other arithmetic  24.7 us (5%)
  matrix products  18.5 us (4%)
  between operations  14.4 us (3%)
  starting transfers between devices  7.9 us (1%)
    all_to_all x4, blocking collectives, to_columns(): lax.all_to_all(values, ('chan', 'bfly'), split_axis=1, concat_axis=0, til...  149 us
    all_to_all x4, blocking collectives, to_rows(): lax.all_to_all(values, ('chan', 'bfly'), split_axis=0, concat_axis=1, til...  138 us
    ppermute x4, waiting for transfers between devices, partner_2(): return lax.ppermute(block, axis, route)  85.8 us
    psum x1, waiting for transfers between devices, local(): lax.psum(all_right.astype(jnp.bfloat16), 'samp').astype(jnp.float32)  31.4 us
    convert_element_type x6, local copies, waits for them, and re-layouts, local(): activation.astype(jnp.float32)  11.5 us
    unnamed x68, local copies, waits for them, and re-layouts  11.5 us
  transfers between devices with their start and end apart: 5, of which 5 were waited for; matrix products, arithmetic and copies ran while one was open for 4% of the time, Pallas kernels for 0%

commit v1 on v0

--- a/solution.py
+++ b/solution.py
@@ -7,14 +7,9 @@
 LAYERS = 2
 
 
-def partner_2(block, axis, distance):
-    count = lax.axis_size(axis)
-    route = []
-    for low in range(count):
-        high = low | 1 << distance
-        if high != low and high < count:
-            route += [(low, high), (high, low)]
-    return lax.ppermute(block, axis, route)
+def flip(values):
+    grouped = values.reshape((BLOCK // 8, 2, 4) + values.shape[1:])
+    return grouped[:, ::-1].reshape(values.shape)
 
 
 def to_columns(values):
@@ -29,6 +24,7 @@
     blocks = right_factor.shape[1]
     samples = features.shape[1]
     height = features.reshape(blocks, BLOCK, samples)
+    mixing = lax.all_to_all(mixing, ("chan", "bfly"), split_axis=3, concat_axis=2, tiled=True)
     saved = []
     for layer_index in range(LAYERS):
         mixed_u = jnp.einsum(
@@ -36,9 +32,9 @@
         ).astype(jnp.bfloat16)
         self_gain = mixing[layer_index, 0][:, :, None]
         cross_gain = mixing[layer_index, 1][:, :, None]
-        partner = partner_2(mixed_u, "bfly", 0)
-        mixed_v = (self_gain * mixed_u + cross_gain * partner).astype(jnp.bfloat16)
-        columns = to_columns(mixed_v)
+        mixed_u = to_columns(mixed_u)
+        partner = flip(mixed_u)
+        columns = (self_gain * mixed_u + cross_gain * partner).astype(jnp.bfloat16)
         kept = (mixed_u, partner)
         outer = jnp.einsum(
             "bjs,jbk->kjs", columns, left_factor[layer_index], preferred_element_type=jnp.float32
@@ -70,7 +66,7 @@
         mixed_u, partner = kept
         self_gain = mixing[layer_index, 0][:, :, None]
         cross_gain = mixing[layer_index, 1][:, :, None]
-        grad_v = to_rows(grad_cols)
+        grad_v = grad_cols
         grad_mix = jnp.stack(
             [
                 jnp.einsum("bjs,bjs->bj", grad_v, mixed_u, preferred_element_type=jnp.float32),
@@ -78,8 +74,8 @@
             ]
         )
         carried = (cross_gain * grad_v).astype(jnp.bfloat16)
-        returned = partner_2(carried, "bfly", 0)
-        grad_u = (self_gain * grad_v + returned.astype(jnp.float32)).astype(jnp.bfloat16)
+        returned = flip(carried)
+        grad_u = to_rows((self_gain * grad_v + returned.astype(jnp.float32)).astype(jnp.bfloat16))
         grad_right = jnp.einsum(
             "bis,bjs->bij", height_in, grad_u, preferred_element_type=jnp.float32
         )
@@ -92,7 +88,9 @@
         mixes[layer_index] = grad_mix
     all_right = jnp.stack(rights)
     all_left = jnp.stack(lefts)
-    all_mix = jnp.stack(mixes)
+    all_mix = lax.all_to_all(
+        jnp.stack(mixes), ("chan", "bfly"), split_axis=2, concat_axis=3, tiled=True
+    )
     all_right, all_left, all_mix = (
         lax.psum(all_right.astype(jnp.bfloat16), "samp").astype(jnp.float32),
         lax.psum(all_left.astype(jnp.bfloat16), "samp").astype(jnp.float32),

time: 528 us -> 500 us (0.947); the launches traced: 527 us -> 490 us
  blocking collectives: 297 us -> 216 us
  local copies, waits for them, and re-layouts: 47.4 us -> 77.5 us
  waiting for transfers between devices: 117 us -> 95.7 us
  starting transfers between devices: 7.9 us -> 28.6 us
  matrix products: 18.5 us -> 32.3 us
    ppermute x4 -> x0, waiting for transfers between devices: 85.8 us -> none  [partner_2(): return lax.ppermute(block, axis, route)]
    all_to_all x0 -> x4, waiting for transfers between devices: none -> 75.6 us  [the longest x1 27.6 us: to_columns(): lax.all_to_all(values, ('chan', 'bfly'), split_axis=1, concat_axis=0, til...]
    all_to_all x4 -> x3, blocking collectives: 149 us -> 104 us  [to_columns(): lax.all_to_all(values, ('chan', 'bfly'), split_axis=1, concat_axis=0, til...]
    all_to_all x4 -> x3, blocking collectives: 138 us -> 104 us  [to_rows(): lax.all_to_all(values, ('chan', 'bfly'), split_axis=0, concat_axis=1, til...]
    all_to_all x0 -> x4, starting transfers between devices: none -> 28.6 us  [the longest x1 13 us: local(): lax.all_to_all(mixing, ('chan', 'bfly'), split_axis=3, concat_axis=2, til...]
    psum x1, waiting for transfers between devices: 31.4 us -> 20.1 us  [local(): lax.psum(all_right.astype(jnp.bfloat16), 'samp').astype(jnp.float32)]
    reshape x0 -> x5, local copies, waits for them, and re-layouts: none -> 10.3 us  [the longest x3 6.87 us: flip(): grouped = values.reshape((BLOCK // 8, 2, 4) + values.shape[1:])]
    all_to_all x4 -> x8, local copies, waits for them, and re-layouts: 2.11 us -> 11.2 us  [to_columns(): lax.all_to_all(values, ('chan', 'bfly'), split_axis=1, concat_axis=0, til...]
  transfers between devices with their start and end apart: 5 -> 5, of which waited for: 5 -> 5; matrix products, arithmetic and copies ran while one was open for 4% -> 5% of each run, Pallas kernels for 0% -> 0%
where the time goes in v1:
time: 500 us; the launch traced here: 490 us
  blocking collectives  216 us (43%)
  waiting for transfers between devices  95.7 us (19%)
  local copies, waits for them, and re-layouts  77.5 us (16%)
  matrix products  32.3 us (6%)
  starting transfers between devices  28.6 us (6%)
  other arithmetic  25.4 us (5%)
  between operations  14.6 us (3%)
    all_to_all x3, blocking collectives, to_columns(): lax.all_to_all(values, ('chan', 'bfly'), split_axis=1, concat_axis=0, til...  104 us
    all_to_all x3, blocking collectives, to_rows(): lax.all_to_all(values, ('chan', 'bfly'), split_axis=0, concat_axis=1, til...  104 us
    all_to_all x1, waiting for transfers between devices, to_columns(): lax.all_to_all(values, ('chan', 'bfly'), split_axis=1, concat_axis=0, til...  27.6 us
    all_to_all x1, waiting for transfers between devices, to_rows(): lax.all_to_all(values, ('chan', 'bfly'), split_axis=0, concat_axis=1, til...  22.8 us
    psum x1, waiting for transfers between devices, local(): lax.psum(all_right.astype(jnp.bfloat16), 'samp').astype(jnp.float32)  20.1 us
    all_to_all x1, waiting for transfers between devices, local(): lax.all_to_all(mixing, ('chan', 'bfly'), split_axis=3, concat_axis=2, til...  15.9 us
    all_to_all x1, starting transfers between devices, local(): lax.all_to_all(mixing, ('chan', 'bfly'), split_axis=3, concat_axis=2, til...  13 us
    convert_element_type x6, local copies, waits for them, and re-layouts, local(): activation.astype(jnp.float32)  11.5 us
  transfers between devices with their start and end apart: 5, of which 5 were waited for; matrix products, arithmetic and copies ran while one was open for 5% of the time, Pallas kernels for 0%

profile of v1, /device:TPU:1, one launch (start us, length us, event | category | flops | bytes accessed | tf_op | source)
XLA Modules:
  0.0 490.4 jit_solution(1854680831663713457)
XLA Ops:
  9.0 13.0 %all-to-all-start = ((f32[2,2,4,256]{2,1,0,3:T(2,128)}), f32[2,2,4,256]{2,1,0,3:T(2,128)S(1)}, u32[]{:S(2)}, u32[]{:S(2)}) async-start(f32[2,2,4,256]{2,1,0,3:T(2,128)} %copy.139), calls=%async_computation | async-start | bytes 1048576 | tf_op jit(solution)/shard_map/all_to_all | solution.py:27
  25.3 15.9 %all-to-all-done = f32[2,2,4,256]{2,1,0,3:T(2,128)S(1)} async-done(((f32[2,2,4,256]{2,1,0,3:T(2,128)}), f32[2,2,4,256]{2,1,0,3:T(2,128)S(1)}, u32[]{:S(2)}, u32[]{:S(2)}) %all-to-all-start) | async-done | bytes 16416 | tf_op jit(solution)/shard_map/all_to_all | solution.py:27
  42.0 4.2 all-to-all-start.1
  47.7 27.6 %all-to-all-done.1 = bf16[4,256,512]{2,0,1:T(4,128)(2,1)S(1)} async-done(((bf16[4,256,512]{2,0,1:T(4,128)(2,1)}), bf16[4,256,512]{2,0,1:T(4,128)(2,1)S(1)}, u32[]{:S(2)}, u32[]{:S(2)}) %all-to-all-start.1) | async-done | bytes 1048608 | tf_op jit(solution)/shard_map/all_to_all | solution.py:16
  78.8 3.6 fusion.20
  84.3 34.5 %all_to_all.153 = bf16[256,4,512]{2,1,0:T(4,128)(2,1)S(1)} all-to-all(bf16[256,4,512]{2,1,0:T(4,128)(2,1)S(1)} %copy.146), channel_id=1, replica_groups=mesh['chan'=32,'bfly'=2,'samp'=4] {'chan','bfly'}, dimensions={0} | all-to-all | bytes 2097152 | tf_op jit(solution)/shard_map/all_to_all | solution.py:20
  128.7 35.1 %all_to_all.154 = bf16[4,256,512]{2,0,1:T(4,128)(2,1)S(1)} all-to-all(bf16[4,256,512]{2,0,1:T(4,128)(2,1)} %copy.150), channel_id=1, replica_groups=mesh['chan'=32,'bfly'=2,'samp'=4] {'chan','bfly'}, dimensions={1} | all-to-all | bytes 2097152 | tf_op jit(solution)/shard_map/all_to_all | solution.py:16
  175.6 3.9 fusion.21
  182.1 34.7 %all_to_all.155 = bf16[256,4,512]{2,1,0:T(4,128)(2,1)S(1)} all-to-all(bf16[256,4,512]{2,1,0:T(4,128)(2,1)} %copy.154), channel_id=1, replica_groups=mesh['chan'=32,'bfly'=2,'samp'=4] {'chan','bfly'}, dimensions={0} | all-to-all | bytes 2097152 | tf_op jit(solution)/shard_map/all_to_all | solution.py:20
  218.8 2.9 reshape.82
  221.7 2.7 fusion.8
  225.3 34.5 %all_to_all.156 = bf16[4,256,512]{2,0,1:T(4,128)(2,1)S(1)} all-to-all(bf16[4,256,512]{2,0,1:T(4,128)(2,1)S(1)} %copy.157), channel_id=1, replica_groups=mesh['chan'=32,'bfly'=2,'samp'=4] {'chan','bfly'}, dimensions={1} | all-to-all | bytes 2097152 | tf_op jit(solution)/shard_map/all_to_all | solution.py:16
  263.3 4.2 fusion.13
  269.6 3.2 reverse_convert_fusion.1
  272.8 3.0 reshape.83
  278.8 34.5 %all_to_all.157 = bf16[256,4,512]{2,1,0:T(4,128)(2,1)S(1)} all-to-all(bf16[256,4,512]{2,1,0:T(4,128)(2,1)S(1)} %copy.159), channel_id=1, replica_groups=mesh['chan'=32,'bfly'=2,'samp'=4] {'chan','bfly'}, dimensions={0} | all-to-all | bytes 2097152 | tf_op jit(solution)/shard_map/all_to_all | solution.py:20
  316.8 4.3 fusion.5
  321.8 34.5 %all_to_all.158 = bf16[4,256,512]{2,0,1:T(4,128)(2,1)S(1)} all-to-all(bf16[4,256,512]{2,0,1:T(4,128)(2,1)S(1)} %copy.161), channel_id=1, replica_groups=mesh['chan'=32,'bfly'=2,'samp'=4] {'chan','bfly'}, dimensions={1} | all-to-all | bytes 2097152 | tf_op jit(solution)/shard_map/all_to_all | solution.py:16
  359.9 4.2 fusion.18
  366.2 3.2 reverse_convert_fusion
  369.4 2.9 reshape.84
  376.3 5.7 %all-to-all-start.8 = ((bf16[256,4,512]{2,1,0:T(4,128)(2,1)}), bf16[256,4,512]{2,1,0:T(4,128)(2,1)}, u32[]{:S(2)}, u32[]{:S(2)}) async-start(bf16[256,4,512]{2,1,0:T(4,128)(2,1)} %copy.163), calls=%async_computation.8 | async-start | bytes 2097152 | tf_op jit(solution)/shard_map/all_to_all | solution.py:20
  382.1 2.7 fusion.28
  388.3 22.8 %all-to-all-done.8 = bf16[256,4,512]{2,1,0:T(4,128)(2,1)} async-done(((bf16[256,4,512]{2,1,0:T(4,128)(2,1)}), bf16[256,4,512]{2,1,0:T(4,128)(2,1)}, u32[]{:S(2)}, u32[]{:S(2)}) %all-to-all-start.8) | async-done | bytes 1048608 | tf_op jit(solution)/shard_map/all_to_all | solution.py:20
  420.4 2.9 reshape.80
  424.3 5.7 %all-to-all-start.9 = ((bf16[2,2,256,4]{3,1,0,2:T(2,128)(2,1)}), bf16[2,2,256,4]{3,1,0,2:T(2,128)(2,1)S(1)}, u32[]{:S(2)}, u32[]{:S(2)}) async-start(bf16[2,2,256,4]{3,1,0,2:T(2,128)(2,1)} %copy.167), calls=%async_computation.9 | async-start | bytes 524288 | tf_op jit(solution)/shard_map/all_to_all | solution.py:91
  430.1 4.6 add_convert_fusion
  434.6 9.3 %all-to-all-done.9 = bf16[2,2,256,4]{3,1,0,2:T(2,128)(2,1)S(1)} async-done(((bf16[2,2,256,4]{3,1,0,2:T(2,128)(2,1)}), bf16[2,2,256,4]{3,1,0,2:T(2,128)(2,1)S(1)}, u32[]{:S(2)}, u32[]{:S(2)}) %all-to-all-start.9) | async-done | bytes 8224 | tf_op jit(solution)/shard_map/all_to_all | solution.py:91
  447.0 8.8 %psum.23 = bf16[2,2,4,256]{3,2,1,0:T(4,128)(2,1)S(1)} all-reduce(bf16[2,2,4,256]{3,2,1,0:T(4,128)(2,1)S(1)} %convert_element_type.248), channel_id=1, replica_groups=mesh['chan'=32,'bfly'=2,'samp'=4] {'samp'}, use_global_device_ids=true, to_apply=%region_2.3 | all-reduce | flops 4096 | bytes 16384 | tf_op jit(solution)/shard_map/psum | solution.py:97
  456.5 2.7 fusion.6
  459.1 20.1 %all-reduce.3.cloned.1.call-done = (bf16[2,4,256,256]{2,3,1,0:T(8,128)(2,1)}, bf16[2,4,256,256]{3,2,1,0:T(8,128)(2,1)}) async-done(((bf16[2,4,256,256]{2,3,1,0:T(8,128)(2,1)}, bf16[2,4,256,256]{3,2,1,0:T(8,128)(2,1)}), (bf16[2,4,256,256]{2,3,1,0:T(8,128)(2,1)}, bf16[2,4,256,256]{3,2,1,0:T(8,128)(2,1)})) %all-reduce.3.cloned.1.call-update) | async-done | bytes 2097168 | tf_op jit(solution)/shard_map/psum | solution.py:95
  479.2 2.7 copy.170
  (90 shorter events, 81.5 us)
Async XLA Ops:
  7.2 14.8 %copy-start = (bf16[1024,512]{1,0:T(8,128)(2,1)S(1)}, bf16[1024,512]{1,0:T(8,128)(2,1)}, u32[]{:S(2)}) copy-start(bf16[1024,512]{1,0:T(8,128)(2,1)} %param.5) | copy-start | bytes 3145732
  9.0 32.2 %all-to-all-start = ((f32[2,2,4,256]{2,1,0,3:T(2,128)}), f32[2,2,4,256]{2,1,0,3:T(2,128)S(1)}, u32[]{:S(2)}, u32[]{:S(2)}) async-start(f32[2,2,4,256]{2,1,0,3:T(2,128)} %copy.139), calls=%async_computation | async-start | bytes 1048576 | tf_op jit(solution)/shard_map/all_to_all | solution.py:27
  41.2 0.8 copy-start.14
  42.0 33.4 %all-to-all-start.1 = ((bf16[4,256,512]{2,0,1:T(4,128)(2,1)}), bf16[4,256,512]{2,0,1:T(4,128)(2,1)S(1)}, u32[]{:S(2)}, u32[]{:S(2)}) async-start(bf16[4,256,512]{2,0,1:T(4,128)(2,1)} %copy.143), calls=%async_computation.1 | async-start | bytes 2097152 | tf_op jit(solution)/shard_map/all_to_all | solution.py:16
  76.0 2.7 copy-start.5
  78.8 3.6 copy-start.7
  121.2 3.4 copy-start.11
  123.6 1.0 copy-start.3
  163.8 1.0 copy-start.2
  376.3 34.8 %all-to-all-start.8 = ((bf16[256,4,512]{2,1,0:T(4,128)(2,1)}), bf16[256,4,512]{2,1,0:T(4,128)(2,1)}, u32[]{:S(2)}, u32[]{:S(2)}) async-start(bf16[256,4,512]{2,1,0:T(4,128)(2,1)} %copy.163), calls=%async_computation.8 | async-start | bytes 2097152 | tf_op jit(solution)/shard_map/all_to_all | solution.py:20
  382.0 97.2 %all-reduce.3.cloned.1.call-start = ((), (), s32[]{:S(2)}) async-start(), calls=%async_computation.10 | async-start | bytes 4194304 | tf_op jit(solution)/shard_map/psum | solution.py:95
  382.0 2.7 copy-start.4
  382.0 2.7 copy-start.9
  382.0 4.0 copy-start.10
  384.7 1.3 copy-start.6
  384.8 1.7 copy-start.8
  415.8 1.8 copy-start.13
  424.3 19.6 %all-to-all-start.9 = ((bf16[2,2,256,4]{3,1,0,2:T(2,128)(2,1)}), bf16[2,2,256,4]{3,1,0,2:T(2,128)(2,1)S(1)}, u32[]{:S(2)}, u32[]{:S(2)}) async-start(bf16[2,2,256,4]{3,1,0,2:T(2,128)(2,1)} %copy.167), calls=%async_computation.9 | async-start | bytes 524288 | tf_op jit(solution)/shard_map/all_to_all | solution.py:91
  430.0 26.4 %copy-start.1 = (bf16[4,256,512]{2,1,0:T(8,128)(2,1)S(1)}, bf16[4,256,512]{2,1,0:T(8,128)(2,1)}, u32[]{:S(2)}) copy-start(bf16[4,256,512]{2,1,0:T(8,128)(2,1)} %all_to_all.141) | copy-start | bytes 3145732
  430.0 26.4 %copy-start.12 = (bf16[2,4,256,256]{3,2,1,0:T(8,128)(2,1)S(1)}, bf16[2,4,256,256]{3,2,1,0:T(8,128)(2,1)}, u32[]{:S(2)}) copy-start(bf16[2,4,256,256]{3,2,1,0:T(8,128)(2,1)} %param.7) | copy-start | bytes 3145732
  479.2 2.7 copy-start.15
Sparse Core Ops, SparseCore 0:
  418.8 60.3 all-reduce.2

commit v2 on v1

v2 whole, which is shorter than its diff:
```python
import functools

import jax
import jax.numpy as jnp
from jax import lax
from jax.experimental import pallas as pl
from jax.experimental.pallas import tpu as pltpu
from jax.sharding import PartitionSpec as P

BLOCK = 256
LAYERS = 2
PEERS = 64
OWN = 4
ROWS = 16
GROUPS = 4
GPEERS = PEERS // GROUPS
SAMP = 4
CHUNKS = 2
MESH = pl.DeviceIdType.MESH
F32 = jnp.float32
BF16 = jnp.bfloat16

U1, T1, U2, COT, T2, DU2, E1, DU1 = range(8)
GL2, GR2, GL1, GR1 = range(4)
Q_ROW, Q_ROW_T, Q_COL, Q_COL_T = range(4)


def mm(a, b):
    return lax.dot_general(a, b, (((1,), (0,)), ((), ())), preferred_element_type=F32)


def mm_t(a, b):
    return lax.dot_general(a, b, (((1,), (1,)), ((), ())), preferred_element_type=F32)


def flip(groups):
    parts = []
    for pair in range(GPEERS // 2):
        parts += [groups[2 * pair + 1 : 2 * pair + 2], groups[2 * pair : 2 * pair + 1]]
    return jnp.concatenate(parts, axis=0)


def kernel(
    feat, cot, right, left, mixing,
    out_hbm, fgrad_hbm, gright_hbm, gleft_hbm, gmix_ref,
    sendb, recvb, qmat, rt, lb, lt, h1, t1, vn, g1, nat, nat2, dvp, coef, outb, fgradb,
    mixs, mixr, gmacc, gms, gm1, gmy, gacc, gsend, rsr, ag,
    a_send, a_recv, m_send, m_recv, r_send, r_recv, g_send, g_recv, o_sem,
):
    samples = h1.shape[3]
    me = lax.axis_index("chan") * 2 + lax.axis_index("bfly")
    y = lax.axis_index("samp")

    def peer_id(p):
        return {"chan": p // 2, "bfly": lax.rem(p, 2)}

    barrier = pltpu.get_barrier_semaphore()

    def greet(k, carry):
        pl.semaphore_signal(barrier, inc=1, device_id=peer_id(lax.rem(me + k, PEERS)), device_id_type=MESH)
        return carry

    lax.fori_loop(1, PEERS, greet, 0)
    for d in range(1, SAMP):
        pl.semaphore_signal(barrier, inc=1, device_id={"samp": lax.rem(y + d, SAMP)}, device_id_type=MESH)

    i0 = lax.broadcasted_iota(jnp.int32, (BLOCK, BLOCK), 0)
    i1 = lax.broadcasted_iota(jnp.int32, (BLOCK, BLOCK), 1)

    def row_of(m):
        return ((m >> 2) & 3) * 64 + (m >> 4) * 4 + (m & 3)

    def col_of(m):
        return (m & 3) * 64 + (m >> 4) * 4 + ((m >> 2) & 3)

    def onehot(mask):
        return jnp.where(mask, 1.0, 0.0).astype(BF16)

    qmat[Q_ROW] = onehot(i1 == row_of(i0))
    qmat[Q_ROW_T] = onehot(i0 == row_of(i1))
    qmat[Q_COL] = onehot(i1 == col_of(i0))
    qmat[Q_COL_T] = onehot(i0 == col_of(i1))

    def to_peers(which, src, put):
        for g in range(GROUPS):
            x = jnp.concatenate([src[b, 64 * g : 64 * g + 64, :] for b in range(OWN)], axis=0)
            put(g, mm(qmat[which], x))

    def put_into(dst):
        def put(g, value):
            dst[GPEERS * g : GPEERS * (g + 1)] = value.astype(BF16).reshape(GPEERS, ROWS, samples)

        return put

    def split_into(dst, g, value):
        value = value.astype(BF16)
        for b in range(OWN):
            dst[b, 64 * g : 64 * g + 64, :] = value[64 * b : 64 * b + 64]

    def from_peers(which, src, dst):
        for g in range(GROUPS):
            x = src[GPEERS * g : GPEERS * (g + 1)].reshape(BLOCK, samples)
            split_into(dst, g, mm(qmat[which], x))

    def chunk_of(c):
        return pl.ds(pl.multiple_of(c * samples, samples), samples)

    def send(a, c):
        def one(k, carry):
            p = lax.rem(me + k, PEERS)
            pltpu.make_async_remote_copy(
                src_ref=sendb.at[a, c, p], dst_ref=recvb.at[a, c, me],
                send_sem=a_send.at[a, c], recv_sem=a_recv.at[a, c],
                device_id=peer_id(p), device_id_type=MESH,
            ).start()
            return carry

        lax.fori_loop(1, PEERS, one, 0)
        recvb[a, c, pl.ds(me, 1)] = sendb[a, c, pl.ds(me, 1)]

    def wait_all(ref, sem):
        pltpu.make_async_copy(ref, ref, sem).wait()

    def wait_recv(a, c):
        wait_all(recvb.at[a, c, pl.ds(0, PEERS - 1)], a_recv.at[a, c])

    pick = onehot((lax.broadcasted_iota(jnp.int32, (BLOCK, 128), 0) & 3) == (lax.broadcasted_iota(jnp.int32, (BLOCK, 128), 1) & 3)).astype(F32)
    lane = lax.broadcasted_iota(jnp.int32, (PEERS, 128), 1)
    owner = lax.broadcasted_iota(jnp.int32, (PEERS, BLOCK), 0)
    unit = lax.broadcasted_iota(jnp.int32, (PEERS, BLOCK), 1)
    message = jnp.zeros((PEERS, 128), F32)
    for r in range(ROWS):
        row = mixing[r // 8, (r // 4) % 2, r % 4 : r % 4 + 1, :]
        spread = jnp.where((unit >> 2) == owner, jnp.broadcast_to(row, (PEERS, BLOCK)), 0.0)
        found = lax.dot_general(
            spread, pick, (((1,), (0,)), ((), ())), precision=lax.Precision.HIGHEST, preferred_element_type=F32
        )
        message = message + jnp.where((lane >> 2) == r, found, 0.0)
    mixs[...] = message.reshape(PEERS, 1, 128)

    def prepare(layer):
        for b in range(OWN):
            rt[layer, b] = right[layer, b].T
            lb[layer, b] = left[layer, b].astype(BF16)
            lt[layer, b] = left[layer, b].T.astype(BF16)

    prepare(0)

    def first(c, carry):
        for b in range(OWN):
            nat[b] = mm(rt[0, b], feat[b, :, chunk_of(c)]).astype(BF16)
        to_peers(Q_ROW, nat, put_into(sendb.at[U1, c]))
        for b in range(OWN):
            nat[b] = cot[b, :, chunk_of(c)]
        to_peers(Q_ROW, nat, put_into(sendb.at[COT, c]))
        return carry

    lax.fori_loop(0, CHUNKS, first, 0)

    pl.semaphore_wait(barrier, PEERS - 1 + SAMP - 1)

    def send_mix(k, carry):
        p = lax.rem(me + k, PEERS)
        pltpu.make_async_remote_copy(
            src_ref=mixs.at[p], dst_ref=mixr.at[me], send_sem=m_send.at[0], recv_sem=m_recv.at[0],
            device_id=peer_id(p), device_id_type=MESH,
        ).start()
        return carry

    lax.fori_loop(1, PEERS, send_mix, 0)
    mixr[pl.ds(me, 1)] = mixs[pl.ds(me, 1)]
    for c in range(CHUNKS):
        send(U1, c)
    prepare(1)
    for a in range(4):
        gacc[a] = jnp.zeros((OWN, BLOCK, BLOCK), F32)
    gmacc[...] = jnp.zeros((PEERS, 128), F32)
    wait_all(mixr.at[pl.ds(0, PEERS - 1)], m_recv.at[0])
    lane3 = lax.broadcasted_iota(jnp.int32, (GPEERS, ROWS, 128), 2)
    row3 = lax.broadcasted_iota(jnp.int32, (GPEERS, ROWS, 128), 1)
    for g in range(GROUPS):
        got = jnp.broadcast_to(mixr[GPEERS * g : GPEERS * (g + 1)], (GPEERS, ROWS, 128))
        for term in range(4):
            value = jnp.sum(jnp.where(lane3 == row3 + ROWS * term, got, 0.0), axis=2, keepdims=True)
            coef[term, GPEERS * g : GPEERS * (g + 1)] = jnp.broadcast_to(value, (GPEERS, ROWS, 128))

    def gain(term, g):
        value = coef[term, GPEERS * g : GPEERS * (g + 1)]
        return jnp.concatenate([value] * (samples // 128), axis=2)

    def mix_forward(layer, a, c):
        for g in range(GROUPS):
            u = recvb[a, c, GPEERS * g : GPEERS * (g + 1)].astype(F32)
            v = (gain(2 * layer, g) * u + gain(2 * layer + 1, g) * flip(u)).astype(BF16)
            split_into(vn.at[layer, c], g, mm(qmat[Q_COL_T], v.reshape(BLOCK, samples)))

    def mix_backward(layer, a, c):
        def put(g, value):
            dv = value.reshape(GPEERS, ROWS, samples)
            dvp[GPEERS * g : GPEERS * (g + 1)] = dv.astype(BF16)
            part = (gain(2 * layer + 1, g) * dv).astype(BF16).astype(F32)
            du = gain(2 * layer, g) * dv + flip(part)
            sendb[a, c, GPEERS * g : GPEERS * (g + 1)] = du.astype(BF16)

        to_peers(Q_COL, nat2, put)

    def mix_gradient(layer, a, c):
        for g in range(GROUPS):
            dv = dvp[GPEERS * g : GPEERS * (g + 1)].astype(F32)
            u = recvb[a, c, GPEERS * g : GPEERS * (g + 1)].astype(F32)
            total = jnp.zeros((GPEERS, ROWS, 128), F32)
            for term, other in ((0, u), (1, flip(u))):
                prod = dv * other
                half = prod[:, :, :128]
                for piece in range(1, samples // 128):
                    half = half + prod[:, :, 128 * piece : 128 * (piece + 1)]
                value = jnp.sum(half, axis=2, keepdims=True)
                total = total + jnp.where(
                    lane3 == row3 + ROWS * (2 * layer + term), jnp.broadcast_to(value, (GPEERS, ROWS, 128)), 0.0
                )
            gmacc[GPEERS * g : GPEERS * (g + 1)] += jnp.sum(total, axis=1)

    def scatter(a):
        gsend[a] = gacc[a].astype(BF16)
        for d in range(1, SAMP):
            to = lax.rem(y + d, SAMP)
            pltpu.make_async_remote_copy(
                src_ref=gsend.at[a, to], dst_ref=rsr.at[a, y], send_sem=r_send.at[a], recv_sem=r_recv.at[a],
                device_id={"samp": to}, device_id_type=MESH,
            ).start()

    def gather(a):
        wait_all(rsr.at[a, pl.ds(0, SAMP - 1)], r_recv.at[a])
        total = gacc[a, y]
        for d in range(1, SAMP):
            total = total + rsr[a, lax.rem(y + d, SAMP)].astype(F32)
        ag[a, y] = total.astype(BF16)
        for d in range(1, SAMP):
            to = lax.rem(y + d, SAMP)
            pltpu.make_async_remote_copy(
                src_ref=ag.at[a, y], dst_ref=ag.at[a, y], send_sem=g_send.at[a], recv_sem=g_recv.at[a],
                device_id={"samp": to}, device_id_type=MESH,
            ).start()

    def store(a):
        wait_all(ag.at[a, pl.ds(0, SAMP - 1)], g_recv.at[a])
        dst = (gleft_hbm if a in (GL1, GL2) else gright_hbm).at[0 if a in (GL1, GR1) else 1]
        pltpu.make_async_copy(ag.at[a], dst, o_sem.at[a]).start()

    def col1(c, carry):
        wait_recv(U1, c)
        mix_forward(0, U1, c)
        for j in range(OWN):
            nat[j] = mm(lt[0, j], vn[0, c, j]).astype(BF16)
        to_peers(Q_COL, nat, put_into(sendb.at[T1, c]))
        send(T1, c)
        send(COT, c)
        return carry

    lax.fori_loop(0, CHUNKS, col1, 0)

    def row2(c, carry):
        wait_recv(T1, c)
        from_peers(Q_ROW_T, recvb.at[T1, c], t1.at[c])
        for b in range(OWN):
            t = t1[c, b].astype(F32)
            h = (feat[b, :, chunk_of(c)].astype(F32) + t * jax.nn.sigmoid(t)).astype(BF16)
            h1[c, b] = h
            nat[b] = mm(rt[1, b], h).astype(BF16)
        to_peers(Q_ROW, nat, put_into(sendb.at[U2, c]))
        send(U2, c)
        return carry

    lax.fori_loop(0, CHUNKS, row2, 0)

    def slope(g, t):
        s = jax.nn.sigmoid(t)
        return (g * s * (1.0 + t * (1.0 - s))).astype(BF16)

    def col2(c, carry):
        wait_recv(COT, c)
        from_peers(Q_COL_T, recvb.at[COT, c], nat2)
        wait_recv(U2, c)
        mix_forward(1, U2, c)
        for j in range(OWN):
            t = mm(lt[1, j], vn[1, c, j]).astype(BF16)
            nat[j] = t
            e = slope(nat2[j].astype(F32), t.astype(F32))
            gacc[GL2, j] += mm_t(vn[1, c, j], e)
            nat2[j] = mm(lb[1, j], e).astype(BF16)
        mix_backward(1, DU2, c)
        send(DU2, c)
        to_peers(Q_COL, nat, put_into(sendb.at[T2, c]))
        send(T2, c)
        mix_gradient(1, U2, c)
        return carry

    lax.fori_loop(0, CHUNKS, col2, 0)
    scatter(GL2)

    def row1(c, carry):
        wait_recv(DU2, c)
        from_peers(Q_ROW_T, recvb.at[DU2, c], nat)
        for b in range(OWN):
            g = (cot[b, :, chunk_of(c)].astype(F32) + mm(right[1, b], nat[b])).astype(BF16)
            g1[c, b] = g
            nat2[b] = slope(g.astype(F32), t1[c, b].astype(F32))
        to_peers(Q_ROW, nat2, put_into(sendb.at[E1, c]))
        send(E1, c)
        for b in range(OWN):
            gacc[GR2, b] += mm_t(h1[c, b], nat[b])
        return carry

    lax.fori_loop(0, CHUNKS, row1, 0)
    gather(GL2)
    scatter(GR2)

    def final_output(c, carry):
        wait_recv(T2, c)
        from_peers(Q_ROW_T, recvb.at[T2, c], nat)
        for b in range(OWN):
            t = nat[b].astype(F32)
            outb[b, :, chunk_of(c)] = (h1[c, b].astype(F32) + t * jax.nn.sigmoid(t)).astype(BF16)
        return carry

    lax.fori_loop(0, CHUNKS, final_output, 0)
    pltpu.make_async_copy(outb, out_hbm, o_sem.at[4]).start()

    def col1_back(c, carry):
        wait_recv(E1, c)
        from_peers(Q_COL_T, recvb.at[E1, c], nat)
        for j in range(OWN):
            nat2[j] = mm(lb[0, j], nat[j]).astype(BF16)
        mix_backward(0, DU1, c)
        send(DU1, c)
        for j in range(OWN):
            gacc[GL1, j] += mm_t(vn[0, c, j], nat[j])
        mix_gradient(0, U1, c)
        return carry

    lax.fori_loop(0, CHUNKS, col1_back, 0)
    scatter(GL1)
    gms[...] = gmacc[...].reshape(PEERS, 1, 128)

    def send_gm(k, carry):
        p = lax.rem(me + k, PEERS)
        pltpu.make_async_remote_copy(
            src_ref=gms.at[p], dst_ref=gm1.at[me], send_sem=m_send.at[1], recv_sem=m_recv.at[1],
            device_id=peer_id(p), device_id_type=MESH,
        ).start()
        return carry

    lax.fori_loop(1, PEERS, send_gm, 0)
    gm1[pl.ds(me, 1)] = gms[pl.ds(me, 1)]
    gather(GR2)
    store(GL2)
    wait_all(gm1.at[pl.ds(0, PEERS - 1)], m_recv.at[1])
    gmy[pl.ds(y, 1)] = gm1[...].reshape(1, PEERS, 1, 128)
    for d in range(1, SAMP):
        to = lax.rem(y + d, SAMP)
        pltpu.make_async_remote_copy(
            src_ref=gm1, dst_ref=gmy.at[y], send_sem=r_send.at[4], recv_sem=r_recv.at[4],
            device_id={"samp": to}, device_id_type=MESH,
        ).start()
    gather(GL1)
    store(GR2)

    def row0(c, carry):
        wait_recv(DU1, c)
        from_peers(Q_ROW_T, recvb.at[DU1, c], dun.at[c])
        for b in range(OWN):
            gacc[GR1, b] += mm_t(feat[b, :, chunk_of(c)], dun[c, b])
        return carry

    dun = h1
    lax.fori_loop(0, CHUNKS, row0, 0)
    scatter(GR1)

    def row0_grad(c, carry):
        for b in range(OWN):
            fgradb[b, :, chunk_of(c)] = (g1[c, b].astype(F32) + mm(right[0, b], dun[c, b])).astype(BF16)
        return carry

    lax.fori_loop(0, CHUNKS, row0_grad, 0)
    pltpu.make_async_copy(fgradb, fgrad_hbm, o_sem.at[5]).start()
    store(GL1)
    wait_all(gmy.at[pl.ds(0, SAMP - 1)], r_recv.at[4])
    gmix_ref[...] = gmy[0] + gmy[1] + gmy[2] + gmy[3]
    gather(GR1)
    store(GR1)

    for a in range(8):
        for c in range(CHUNKS):
            wait_all(sendb.at[a, c, pl.ds(0, PEERS - 1)], a_send.at[a, c])
    wait_all(mixs.at[pl.ds(0, PEERS - 1)], m_send.at[0])
    wait_all(gms.at[pl.ds(0, PEERS - 1)], m_send.at[1])
    for a in range(4):
        wait_all(gsend.at[a, pl.ds(0, SAMP - 1)], r_send.at[a])
        wait_all(ag.at[a, pl.ds(0, SAMP - 1)], g_send.at[a])
        wait_all(ag.at[a], o_sem.at[a])
    wait_all(gmy.at[pl.ds(0, SAMP - 1)], r_send.at[4])
    wait_all(outb, o_sem.at[4])
    wait_all(fgradb, o_sem.at[5])


def local(features, cotangent, right_factor, left_factor, mixing):
    width = features.shape[1]
    samples = width // CHUNKS
    vmem = pl.BlockSpec(memory_space=pltpu.VMEM)
    hbm = pl.BlockSpec(memory_space=pl.ANY)
    acts = jax.ShapeDtypeStruct((OWN, BLOCK, width), BF16)
    grads = jax.ShapeDtypeStruct((LAYERS, OWN, BLOCK, BLOCK), BF16)
    chunked = pltpu.VMEM((CHUNKS, OWN, BLOCK, samples), BF16)
    small = pltpu.VMEM((PEERS, 1, 128), F32)
    output, fgrad, gright, gleft, gmix = pl.pallas_call(
        kernel,
        out_shape=(acts, acts, grads, grads, jax.ShapeDtypeStruct((PEERS, 1, 128), F32)),
        in_specs=[vmem] * 5,
        out_specs=(hbm, hbm, hbm, hbm, vmem),
        scratch_shapes=[
            pltpu.VMEM((8, CHUNKS, PEERS, ROWS, samples), BF16),
            pltpu.VMEM((8, CHUNKS, PEERS, ROWS, samples), BF16),
            pltpu.VMEM((4, BLOCK, BLOCK), BF16),
            pltpu.VMEM((LAYERS, OWN, BLOCK, BLOCK), BF16),
            pltpu.VMEM((LAYERS, OWN, BLOCK, BLOCK), BF16),
            pltpu.VMEM((LAYERS, OWN, BLOCK, BLOCK), BF16),
            chunked,
            chunked,
            pltpu.VMEM((LAYERS, CHUNKS, OWN, BLOCK, samples), BF16),
            chunked,
            pltpu.VMEM((OWN, BLOCK, samples), BF16),
            pltpu.VMEM((OWN, BLOCK, samples), BF16),
            pltpu.VMEM((PEERS, ROWS, samples), BF16),
            pltpu.VMEM((4, PEERS, ROWS, 128), F32),
            pltpu.VMEM((OWN, BLOCK, width), BF16),
            pltpu.VMEM((OWN, BLOCK, width), BF16),
            small,
            small,
            pltpu.VMEM((PEERS, 128), F32),
            small,
            small,
            pltpu.VMEM((SAMP, PEERS, 1, 128), F32),
            pltpu.VMEM((4, OWN, BLOCK, BLOCK), F32),
            pltpu.VMEM((4, OWN, BLOCK, BLOCK), BF16),
            pltpu.VMEM((4, SAMP, BLOCK, BLOCK), BF16),
            pltpu.VMEM((4, SAMP, BLOCK, BLOCK), BF16),
            pltpu.SemaphoreType.DMA((8, CHUNKS)),
            pltpu.SemaphoreType.DMA((8, CHUNKS)),
            pltpu.SemaphoreType.DMA((2,)),
            pltpu.SemaphoreType.DMA((2,)),
            pltpu.SemaphoreType.DMA((5,)),
            pltpu.SemaphoreType.DMA((5,)),
            pltpu.SemaphoreType.DMA((4,)),
            pltpu.SemaphoreType.DMA((4,)),
            pltpu.SemaphoreType.DMA((6,)),
        ],
        compiler_params=pltpu.CompilerParams(
            collective_id=0, has_side_effects=True, vmem_limit_bytes=58 * 1024 * 1024
        ),
    )(
        features.reshape(OWN, BLOCK, width),
        cotangent.reshape(OWN, BLOCK, width),
        right_factor,
        left_factor,
        mixing,
    )
    gmix = gmix.reshape(PEERS, 128)[:, :64].reshape(PEERS, LAYERS, 2, OWN, OWN)
    gmix = gmix.transpose(1, 2, 3, 0, 4).reshape(LAYERS, 2, OWN, BLOCK)
    return (
        output.reshape(OWN * BLOCK, width),
        fgrad.reshape(OWN * BLOCK, width),
        gright.astype(F32),
        gleft.astype(F32),
        gmix,
    )


def solution(mesh):
    specs = (
        P(("chan", "bfly"), "samp"),
        P(("chan", "bfly"), "samp"),
        P(None, ("chan", "bfly"), None, None),
        P(None, ("chan", "bfly"), None, None),
        P(None, None, ("chan", "bfly"), None),
    )
    return jax.shard_map(local, mesh=mesh, in_specs=specs, out_specs=specs, check_vma=False)
```

time: 500 us -> 232 us (0.46); the launches traced: 490 us -> 232 us
  Pallas kernels: 0 us -> 223 us
  blocking collectives: 216 us -> 0 us
  waiting for transfers between devices: 95.7 us -> 0 us
  local copies, waits for them, and re-layouts: 77.5 us -> 3.93 us
  matrix products: 32.3 us -> 0 us
  starting transfers between devices: 28.6 us -> 0 us
  other arithmetic: 25.4 us -> 4.24 us
  between operations: 14.6 us -> 0.66 us
    pallas_call x0 -> x1, Pallas kernels: none -> 223 us  [local(): pl.pallas_call(kernel, out_shape=(acts, acts, grads, grads, jax.ShapeDtyp...]
    all_to_all x6 -> x0, blocking collectives: 208 us -> none  [the longest x3 104 us: to_columns(): lax.all_to_all(values, ('chan', 'bfly'), split_axis=1, concat_axis=0, til...]
    all_to_all x4 -> x0, waiting for transfers between devices: 75.6 us -> none  [the longest x1 27.6 us: to_columns(): lax.all_to_all(values, ('chan', 'bfly'), split_axis=1, concat_axis=0, til...]
    convert_element_type x19 -> x0, local copies, waits for them, and re-layouts: 33.4 us -> none  [the longest x6 11.5 us: local(): activation.astype(jnp.float32)]
    dot_general x12 -> x0, matrix products: 32.3 us -> none  [the longest x2 8.45 us: local(): jnp.einsum('jbk,kjs->bjs', left_factor[layer_index], error_cols, preferre...]
    all_to_all x4 -> x0, starting transfers between devices: 28.6 us -> none  [the longest x1 13 us: local(): lax.all_to_all(mixing, ('chan', 'bfly'), split_axis=3, concat_axis=2, til...]
    all_to_all x15 -> x0, local copies, waits for them, and re-layouts: 21.2 us -> none  [the longest x8 11.2 us: to_columns(): lax.all_to_all(values, ('chan', 'bfly'), split_axis=1, concat_axis=0, til...]
    psum x1 -> x0, waiting for transfers between devices: 20.1 us -> none  [local(): lax.psum(all_right.astype(jnp.bfloat16), 'samp').astype(jnp.float32)]
  transfers between devices with their start and end apart: 5 -> 0, of which waited for: 5 -> 0; matrix products, arithmetic and copies ran while one was open for 5% -> 0% of each run, Pallas kernels for 0% -> 0%
where the time goes in v2:
time: 232 us
  Pallas kernels  223 us (96%)
  other arithmetic  4.24 us (2%)
  local copies, waits for them, and re-layouts  3.93 us (2%)
    pallas_call x1, Pallas kernels, local(): pl.pallas_call(kernel, out_shape=(acts, acts, grads, grads, jax.ShapeDtyp...  223 us

profile of v2, /device:TPU:1, one launch (start us, length us, event | category | flops | bytes accessed | tf_op | source)
XLA Modules:
  0.0 231.8 jit_solution(9350235625625246800)
XLA Ops:
  0.6 222.9 %shard_map.92 = (bf16[4,256,512]{2,1,0:T(8,128)(2,1)}, bf16[4,256,512]{2,1,0:T(8,128)(2,1)}, bf16[2,4,256,256]{3,2,1,0:T(8,128)(2,1)}, bf16[2,4,256,256]{3,2,1,0:T(8,128)(2,1)}, f32[64,1,128]{2,1,0:T(1,128)}) custom-call(bf16[4,256,512]{2,1,0:T(8,128)(2,1)} %bitcast.11, bf16[4,256,512]{2,1,0:T(8,128)(2,1)} %bitcast.12, bf16[2,4,256,256]{3,2,1,0:T(8,128)(2,1)} %right.1, ...), custom_call_target="tpu_custom_call" | custom-call | tf_op jit(solution)/shard_map/pallas_call | solution.py:415
  223.6 0.8 copy.11
  224.4 0.0 copy-start
  224.4 0.2 copy.12
  224.7 0.9 reshape.37
  225.6 2.7 %convert_element_type.6 = f32[2,4,256,256]{3,2,1,0:T(8,128)} convert(bf16[2,4,256,256]{3,2,1,0:T(8,128)(2,1)} %get-tuple-element.12) | non-fusion elementwise | flops 524288 | bytes 3145728 | tf_op jit(solution)/shard_map/convert_element_type | solution.py:472
  228.3 0.0 copy-done
  228.3 0.0 copy-start.2
  228.3 0.0 copy-start.1
  228.3 1.5 convert_element_type.7
  229.8 0.0 copy-done.2
  229.8 1.0 copy.15
  230.8 0.0 copy-done.1
  230.8 1.0 copy.16
Async XLA Ops:
  224.4 3.9 %copy-start = (bf16[2,4,256,256]{3,2,1,0:T(8,128)(2,1)S(1)}, bf16[2,4,256,256]{3,2,1,0:T(8,128)(2,1)}, u32[]{:S(2)}) copy-start(bf16[2,4,256,256]{3,2,1,0:T(8,128)(2,1)} %get-tuple-element.13) | copy-start | bytes 3145732
  228.3 1.5 copy-start.2
  228.3 2.5 %copy-start.1 = (bf16[4,256,512]{2,1,0:T(8,128)(2,1)S(1)}, bf16[4,256,512]{2,1,0:T(8,128)(2,1)}, u32[]{:S(2)}) copy-start(bf16[4,256,512]{2,1,0:T(8,128)(2,1)} %get-tuple-element.11) | copy-start | bytes 3145732

commit v3 on v2

--- a/solution.py
+++ b/solution.py
@@ -16,6 +16,10 @@
 GPEERS = PEERS // GROUPS
 SAMP = 4
 CHUNKS = 2
+EARLY = 40
+LATE = 17
+SPLIT = 33
+FINAL = 4
 MESH = pl.DeviceIdType.MESH
 F32 = jnp.float32
 BF16 = jnp.bfloat16
@@ -41,16 +45,30 @@
 
 
 def kernel(
-    feat, cot, right, left, mixing,
+    feat_hbm, cot_hbm, right_hbm, left_hbm, mixing,
     out_hbm, fgrad_hbm, gright_hbm, gleft_hbm, gmix_ref,
-    sendb, recvb, qmat, rt, lb, lt, h1, t1, vn, g1, nat, nat2, dvp, coef, outb, fgradb,
+    feat, cot, right, left, sendb, recvb, qmat, rt, lb, lt, h1, h1d, t1, vn, g1, nat, nat2, dvp, coef, outb, fgradb,
     mixs, mixr, gmacc, gms, gm1, gmy, gacc, gsend, rsr, ag,
-    a_send, a_recv, m_send, m_recv, r_send, r_recv, g_send, g_recv, o_sem,
+    a_send, a_recv, m_send, m_recv, r_send, r_recv, g_send, g_recv, o_sem, i_sem,
 ):
     samples = h1.shape[3]
     me = lax.axis_index("chan") * 2 + lax.axis_index("bfly")
     y = lax.axis_index("samp")
 
+    def fetch(n, src, dst):
+        return pltpu.make_async_copy(src, dst, i_sem.at[n])
+
+    fetches = [
+        fetch(0, right_hbm.at[0], right.at[0]),
+        fetch(1, feat_hbm, feat),
+        fetch(2, cot_hbm, cot),
+        fetch(3, left_hbm.at[0], left.at[0]),
+        fetch(4, right_hbm.at[1], right.at[1]),
+        fetch(5, left_hbm.at[1], left.at[1]),
+    ]
+    for one_fetch in fetches:
+        one_fetch.start()
+
     def peer_id(p):
         return {"chan": p // 2, "bfly": lax.rem(p, 2)}
 
@@ -77,9 +95,6 @@
         return jnp.where(mask, 1.0, 0.0).astype(BF16)
 
     qmat[Q_ROW] = onehot(i1 == row_of(i0))
-    qmat[Q_ROW_T] = onehot(i0 == row_of(i1))
-    qmat[Q_COL] = onehot(i1 == col_of(i0))
-    qmat[Q_COL_T] = onehot(i0 == col_of(i1))
 
     def to_peers(which, src, put):
         for g in range(GROUPS):
@@ -105,7 +120,7 @@
     def chunk_of(c):
         return pl.ds(pl.multiple_of(c * samples, samples), samples)
 
-    def send(a, c):
+    def send(a, c, low=1, high=PEERS):
         def one(k, carry):
             p = lax.rem(me + k, PEERS)
             pltpu.make_async_remote_copy(
@@ -115,14 +130,30 @@
             ).start()
             return carry
 
-        lax.fori_loop(1, PEERS, one, 0)
-        recvb[a, c, pl.ds(me, 1)] = sendb[a, c, pl.ds(me, 1)]
+        lax.fori_loop(low, high, one, 0)
+        if low == 1:
+            recvb[a, c, pl.ds(me, 1)] = sendb[a, c, pl.ds(me, 1)]
 
     def wait_all(ref, sem):
         pltpu.make_async_copy(ref, ref, sem).wait()
 
     def wait_recv(a, c):
         wait_all(recvb.at[a, c, pl.ds(0, PEERS - 1)], a_recv.at[a, c])
+
+    def first(c):
+        for b in range(OWN):
+            nat[b] = mm(rt[0, b], feat[b, :, chunk_of(c)]).astype(BF16)
+        to_peers(Q_ROW, nat, put_into(sendb.at[U1, c]))
+
+    fetches[0].wait()
+    for b in range(OWN):
+        rt[0, b] = right[0, b].T
+    fetches[1].wait()
+    first(0)
+
+    pl.semaphore_wait(barrier, PEERS - 1 + SAMP - 1)
+
+    send(U1, 0)
 
     pick = onehot((lax.broadcasted_iota(jnp.int32, (BLOCK, 128), 0) & 3) == (lax.broadcasted_iota(jnp.int32, (BLOCK, 128), 1) & 3)).astype(F32)
     lane = lax.broadcasted_iota(jnp.int32, (PEERS, 128), 1)
@@ -138,27 +169,6 @@
         message = message + jnp.where((lane >> 2) == r, found, 0.0)
     mixs[...] = message.reshape(PEERS, 1, 128)
 
-    def prepare(layer):
-        for b in range(OWN):
-            rt[layer, b] = right[layer, b].T
-            lb[layer, b] = left[layer, b].astype(BF16)
-            lt[layer, b] = left[layer, b].T.astype(BF16)
-
-    prepare(0)
-
-    def first(c, carry):
-        for b in range(OWN):
-            nat[b] = mm(rt[0, b], feat[b, :, chunk_of(c)]).astype(BF16)
-        to_peers(Q_ROW, nat, put_into(sendb.at[U1, c]))
-        for b in range(OWN):
-            nat[b] = cot[b, :, chunk_of(c)]
-        to_peers(Q_ROW, nat, put_into(sendb.at[COT, c]))
-        return carry
-
-    lax.fori_loop(0, CHUNKS, first, 0)
-
-    pl.semaphore_wait(barrier, PEERS - 1 + SAMP - 1)
-
     def send_mix(k, carry):
         p = lax.rem(me + k, PEERS)
         pltpu.make_async_remote_copy(
@@ -169,9 +179,25 @@
 
     lax.fori_loop(1, PEERS, send_mix, 0)
     mixr[pl.ds(me, 1)] = mixs[pl.ds(me, 1)]
+    for c in range(1, CHUNKS):
+        first(c)
+        send(U1, c)
+
+    qmat[Q_ROW_T] = onehot(i0 == row_of(i1))
+    qmat[Q_COL] = onehot(i1 == col_of(i0))
+    qmat[Q_COL_T] = onehot(i0 == col_of(i1))
+    fetches[2].wait()
     for c in range(CHUNKS):
-        send(U1, c)
-    prepare(1)
+        for b in range(OWN):
+            nat[b] = cot[b, :, chunk_of(c)]
+        to_peers(Q_ROW, nat, put_into(sendb.at[COT, c]))
+    for n in (3, 4, 5):
+        fetches[n].wait()
+    for b in range(OWN):
+        rt[1, b] = right[1, b].T
+        for layer in range(LAYERS):
+            lb[layer, b] = left[layer, b].astype(BF16)
+            lt[layer, b] = left[layer, b].T.astype(BF16)
     for a in range(4):
         gacc[a] = jnp.zeros((OWN, BLOCK, BLOCK), F32)
     gmacc[...] = jnp.zeros((PEERS, 128), F32)
@@ -291,12 +317,12 @@
         mix_backward(1, DU2, c)
         send(DU2, c)
         to_peers(Q_COL, nat, put_into(sendb.at[T2, c]))
-        send(T2, c)
         mix_gradient(1, U2, c)
         return carry
 
     lax.fori_loop(0, CHUNKS, col2, 0)
     scatter(GL2)
+    send(T2, 0, 1, EARLY)
 
     def row1(c, carry):
         wait_recv(DU2, c)
@@ -315,31 +341,28 @@
     gather(GL2)
     scatter(GR2)
 
-    def final_output(c, carry):
-        wait_recv(T2, c)
-        from_peers(Q_ROW_T, recvb.at[T2, c], nat)
-        for b in range(OWN):
-            t = nat[b].astype(F32)
-            outb[b, :, chunk_of(c)] = (h1[c, b].astype(F32) + t * jax.nn.sigmoid(t)).astype(BF16)
-        return carry
-
-    lax.fori_loop(0, CHUNKS, final_output, 0)
-    pltpu.make_async_copy(outb, out_hbm, o_sem.at[4]).start()
-
-    def col1_back(c, carry):
+    def col1_back(c):
         wait_recv(E1, c)
         from_peers(Q_COL_T, recvb.at[E1, c], nat)
         for j in range(OWN):
             nat2[j] = mm(lb[0, j], nat[j]).astype(BF16)
         mix_backward(0, DU1, c)
-        send(DU1, c)
+
+    def col1_grad(c):
         for j in range(OWN):
             gacc[GL1, j] += mm_t(vn[0, c, j], nat[j])
-        mix_gradient(0, U1, c)
-        return carry
-
-    lax.fori_loop(0, CHUNKS, col1_back, 0)
+
+    col1_back(0)
+    send(DU1, 0)
+    col1_grad(0)
+    mix_gradient(0, U1, 0)
+    gather(GR2)
+    store(GL2)
+    col1_back(1)
+    col1_grad(1)
     scatter(GL1)
+    send(DU1, 1, 1, SPLIT)
+    mix_gradient(0, U1, 1)
     gms[...] = gmacc[...].reshape(PEERS, 1, 128)
 
     def send_gm(k, carry):
@@ -352,8 +375,21 @@
 
     lax.fori_loop(1, PEERS, send_gm, 0)
     gm1[pl.ds(me, 1)] = gms[pl.ds(me, 1)]
-    gather(GR2)
-    store(GL2)
+    gather(GL1)
+    send(DU1, 1, SPLIT, PEERS)
+    store(GR2)
+
+    dun = h1d
+
+    def row0(c, carry):
+        wait_recv(DU1, c)
+        from_peers(Q_ROW_T, recvb.at[DU1, c], dun.at[c])
+        for b in range(OWN):
+            gacc[GR1, b] += mm_t(feat[b, :, chunk_of(c)], dun[c, b])
+        return carry
+
+    lax.fori_loop(0, CHUNKS, row0, 0)
+    scatter(GR1)
     wait_all(gm1.at[pl.ds(0, PEERS - 1)], m_recv.at[1])
     gmy[pl.ds(y, 1)] = gm1[...].reshape(1, PEERS, 1, 128)
     for d in range(1, SAMP):
@@ -362,19 +398,9 @@
             src_ref=gm1, dst_ref=gmy.at[y], send_sem=r_send.at[4], recv_sem=r_recv.at[4],
             device_id={"samp": to}, device_id_type=MESH,
         ).start()
-    gather(GL1)
-    store(GR2)
-
-    def row0(c, carry):
-        wait_recv(DU1, c)
-        from_peers(Q_ROW_T, recvb.at[DU1, c], dun.at[c])
-        for b in range(OWN):
-            gacc[GR1, b] += mm_t(feat[b, :, chunk_of(c)], dun[c, b])
-        return carry
-
-    dun = h1
-    lax.fori_loop(0, CHUNKS, row0, 0)
-    scatter(GR1)
+    if EARLY < PEERS:
+        send(T2, 0, EARLY, PEERS)
+    send(T2, 1, 1, LATE)
 
     def row0_grad(c, carry):
         for b in range(OWN):
@@ -384,9 +410,32 @@
     lax.fori_loop(0, CHUNKS, row0_grad, 0)
     pltpu.make_async_copy(fgradb, fgrad_hbm, o_sem.at[5]).start()
     store(GL1)
+    gather(GR1)
+    send(T2, 1, LATE, PEERS)
     wait_all(gmy.at[pl.ds(0, SAMP - 1)], r_recv.at[4])
-    gmix_ref[...] = gmy[0] + gmy[1] + gmy[2] + gmy[3]
-    gather(GR1)
+    total = (gmy[0] + gmy[1] + gmy[2] + gmy[3]).reshape(PEERS, 128)
+    spread_back = onehot(
+        (lax.broadcasted_iota(jnp.int32, (128, BLOCK), 0) & 3) == (lax.broadcasted_iota(jnp.int32, (128, BLOCK), 1) & 3)
+    ).astype(F32)
+    for r in range(ROWS):
+        found = lax.dot_general(
+            jnp.where((lane >> 2) == r, total, 0.0), spread_back, (((1,), (0,)), ((), ())),
+            precision=lax.Precision.HIGHEST, preferred_element_type=F32,
+        )
+        gmix_ref[r // 8, (r // 4) % 2, r % 4 : r % 4 + 1, :] = jnp.sum(
+            jnp.where((unit >> 2) == owner, found, 0.0), axis=0, keepdims=True
+        )
+
+    def final_output(c, carry):
+        wait_recv(T2, c)
+        from_peers(Q_ROW_T, recvb.at[T2, c], nat)
+        for b in range(OWN):
+            t = nat[b].astype(F32)
+            outb[b, :, chunk_of(c)] = (h1[c, b].astype(F32) + t * jax.nn.sigmoid(t)).astype(BF16)
+        return carry
+
+    lax.fori_loop(0, CHUNKS, final_output, 0)
+    pltpu.make_async_copy(outb, out_hbm, o_sem.at[4]).start()
     store(GR1)
 
     for a in range(8):
@@ -403,6 +452,14 @@
     wait_all(fgradb, o_sem.at[5])
 
 
+def finish(out_in, fgrad_in, gright_in, gleft_in, gmix_in, out, fgrad, gright, gleft, gmix):
+    out[...] = out_in[...]
+    fgrad[...] = fgrad_in[...]
+    gright[...] = gright_in[...].astype(F32)
+    gleft[...] = gleft_in[...].astype(F32)
+    gmix[...] = gmix_in[...]
+
+
 def local(features, cotangent, right_factor, left_factor, mixing):
     width = features.shape[1]
     samples = width // CHUNKS
@@ -414,16 +471,21 @@
     small = pltpu.VMEM((PEERS, 1, 128), F32)
     output, fgrad, gright, gleft, gmix = pl.pallas_call(
         kernel,
-        out_shape=(acts, acts, grads, grads, jax.ShapeDtypeStruct((PEERS, 1, 128), F32)),
-        in_specs=[vmem] * 5,
+        out_shape=(acts, acts, grads, grads, jax.ShapeDtypeStruct((LAYERS, 2, OWN, BLOCK), F32)),
+        in_specs=[hbm] * 4 + [vmem],
         out_specs=(hbm, hbm, hbm, hbm, vmem),
         scratch_shapes=[
+            pltpu.VMEM((OWN, BLOCK, width), BF16),
+            pltpu.VMEM((OWN, BLOCK, width), BF16),
+            pltpu.VMEM((LAYERS, OWN, BLOCK, BLOCK), BF16),
+            pltpu.VMEM((LAYERS, OWN, BLOCK, BLOCK), F32),
             pltpu.VMEM((8, CHUNKS, PEERS, ROWS, samples), BF16),
             pltpu.VMEM((8, CHUNKS, PEERS, ROWS, samples), BF16),
             pltpu.VMEM((4, BLOCK, BLOCK), BF16),
             pltpu.VMEM((LAYERS, OWN, BLOCK, BLOCK), BF16),
             pltpu.VMEM((LAYERS, OWN, BLOCK, BLOCK), BF16),
             pltpu.VMEM((LAYERS, OWN, BLOCK, BLOCK), BF16),
+            chunked,
             chunked,
             chunked,
             pltpu.VMEM((LAYERS, CHUNKS, OWN, BLOCK, samples), BF16),
@@ -453,6 +515,7 @@
             pltpu.SemaphoreType.DMA((4,)),
             pltpu.SemaphoreType.DMA((4,)),
             pltpu.SemaphoreType.DMA((6,)),
+            pltpu.SemaphoreType.DMA((6,)),
         ],
         compiler_params=pltpu.CompilerParams(
             collective_id=0, has_side_effects=True, vmem_limit_bytes=58 * 1024 * 1024
@@ -464,15 +527,28 @@
         left_factor,
         mixing,
     )
-    gmix = gmix.reshape(PEERS, 128)[:, :64].reshape(PEERS, LAYERS, 2, OWN, OWN)
-    gmix = gmix.transpose(1, 2, 3, 0, 4).reshape(LAYERS, 2, OWN, BLOCK)
-    return (
-        output.reshape(OWN * BLOCK, width),
-        fgrad.reshape(OWN * BLOCK, width),
-        gright.astype(F32),
-        gleft.astype(F32),
-        gmix,
-    )
+    rows = OWN * BLOCK
+    step = rows // FINAL
+    blocks = LAYERS * OWN // FINAL
+    wide = pl.BlockSpec((step, width), lambda i: (i, 0))
+    block = pl.BlockSpec((blocks, BLOCK, BLOCK), lambda i: (i, 0, 0))
+    whole = pl.BlockSpec((LAYERS, 2, OWN, BLOCK), lambda i: (0, 0, 0, 0))
+    flat = (LAYERS * OWN, BLOCK, BLOCK)
+    output, fgrad, gright, gleft, gmix = pl.pallas_call(
+        finish,
+        grid=(FINAL,),
+        out_shape=(
+            jax.ShapeDtypeStruct((rows, width), BF16),
+            jax.ShapeDtypeStruct((rows, width), BF16),
+            jax.ShapeDtypeStruct(flat, F32),
+            jax.ShapeDtypeStruct(flat, F32),
+            jax.ShapeDtypeStruct((LAYERS, 2, OWN, BLOCK), F32),
+        ),
+        in_specs=[wide, wide, block, block, whole],
+        out_specs=(wide, wide, block, block, whole),
+    )(output.reshape(rows, width), fgrad.reshape(rows, width), gright.reshape(flat), gleft.reshape(flat), gmix)
+    shape = (LAYERS, OWN, BLOCK, BLOCK)
+    return output, fgrad, gright.reshape(shape), gleft.reshape(shape), gmix
 
 
 def solution(mesh):

time: 232 us -> 211 us (0.909)
  Pallas kernels: 223 us -> 210 us
  other arithmetic: 4.24 us -> 0 us
  local copies, waits for them, and re-layouts: 3.93 us -> 0 us
    pallas_call x1, Pallas kernels: 223 us -> 205 us  [local(): pl.pallas_call(kernel, out_shape=(acts, acts, grads, grads, jax.ShapeDtyp...]
    pallas_call x0 -> x1, Pallas kernels: none -> 5.25 us  [local(): pl.pallas_call(finish, grid=(FINAL,), out_shape=(jax.ShapeDtypeStruct((ro...]
    convert_element_type x2 -> x0, other arithmetic: 4.24 us -> none  [the longest x1 2.73 us: local(): gright.astype(F32)]
where the time goes in v3:
time: 211 us; the launch traced here: 210 us
  Pallas kernels  210 us (100%)
    pallas_call x1, Pallas kernels, local(): pl.pallas_call(kernel, out_shape=(acts, acts, grads, grads, jax.ShapeDtyp...  205 us
    pallas_call x1, Pallas kernels, local(): pl.pallas_call(finish, grid=(FINAL,), out_shape=(jax.ShapeDtypeStruct((ro...  5.25 us

profile of v3, /device:TPU:1, one launch (start us, length us, event | category | flops | bytes accessed | tf_op | source)
XLA Modules:
  0.0 210.5 jit_solution(10507762754266854972)
XLA Ops:
  0.6 204.6 %shard_map.92 = (bf16[4,256,512]{2,1,0:T(8,128)(2,1)}, bf16[4,256,512]{2,1,0:T(8,128)(2,1)}, bf16[2,4,256,256]{3,2,1,0:T(8,128)(2,1)}, bf16[2,4,256,256]{3,2,1,0:T(8,128)(2,1)}, f32[2,2,4,256]{3,2,1,0:T(4,128)}) custom-call(bf16[4,256,512]{2,1,0:T(8,128)(2,1)} %bitcast.8, bf16[4,256,512]{2,1,0:T(8,128)(2,1)} %bitcast.9, bf16[2,4,256,256]{3,2,1,0:T(8,128)(2,1)} %right_hbm.1, ...), custom_call_target="tpu_custom_call" | custom-call | tf_op jit(solution)/shard_map/pallas_call | solution.py:472
  205.2 5.3 %shard_map.93 = (bf16[1024,512]{1,0:T(8,128)(2,1)}, bf16[1024,512]{1,0:T(8,128)(2,1)}, f32[8,256,256]{2,1,0:T(8,128)}, f32[8,256,256]{2,1,0:T(8,128)}, f32[2,2,4,256]{3,2,1,0:T(4,128)}) custom-call(bf16[1024,512]{1,0:T(8,128)(2,1)} %bitcast.10, bf16[1024,512]{1,0:T(8,128)(2,1)} %bitcast.11, bf16[8,256,256]{2,1,0:T(8,128)(2,1)} %bitcast.12, ...), custom_call_target="tpu_custom_call" | custom-call | tf_op jit(solution)/shard_map/pallas_call | solution.py:537

commit v4 on v3

--- a/solution.py
+++ b/solution.py
@@ -19,7 +19,6 @@
 EARLY = 40
 LATE = 17
 SPLIT = 33
-FINAL = 4
 MESH = pl.DeviceIdType.MESH
 F32 = jnp.float32
 BF16 = jnp.bfloat16
@@ -45,9 +44,9 @@
 
 
 def kernel(
-    feat_hbm, cot_hbm, right_hbm, left_hbm, mixing,
+    feat_hbm, cot_hbm, right_hbm, left_hbm, mixing_hbm,
     out_hbm, fgrad_hbm, gright_hbm, gleft_hbm, gmix_ref,
-    feat, cot, right, left, sendb, recvb, qmat, rt, lb, lt, h1, h1d, t1, vn, g1, nat, nat2, dvp, coef, outb, fgradb,
+    feat, cot, right, left, mixing, sendb, recvb, qmat, rt, lb, lt, h1, h1d, t1, vn, g1, nat, nat2, dvp, coef, outb, fgradb,
     mixs, mixr, gmacc, gms, gm1, gmy, gacc, gsend, rsr, ag,
     a_send, a_recv, m_send, m_recv, r_send, r_recv, g_send, g_recv, o_sem, i_sem,
 ):
@@ -59,15 +58,17 @@
         return pltpu.make_async_copy(src, dst, i_sem.at[n])
 
     fetches = [
+        fetch(2, cot_hbm, cot),
         fetch(0, right_hbm.at[0], right.at[0]),
         fetch(1, feat_hbm, feat),
-        fetch(2, cot_hbm, cot),
         fetch(3, left_hbm.at[0], left.at[0]),
         fetch(4, right_hbm.at[1], right.at[1]),
         fetch(5, left_hbm.at[1], left.at[1]),
+        fetch(6, mixing_hbm, mixing),
     ]
     for one_fetch in fetches:
         one_fetch.start()
+    fetches = [fetches[1], fetches[2], fetches[0]] + fetches[3:]
 
     def peer_id(p):
         return {"chan": p // 2, "bfly": lax.rem(p, 2)}
@@ -145,20 +146,27 @@
             nat[b] = mm(rt[0, b], feat[b, :, chunk_of(c)]).astype(BF16)
         to_peers(Q_ROW, nat, put_into(sendb.at[U1, c]))
 
+    def first_cot(c):
+        for b in range(OWN):
+            nat2[b] = cot[b, :, chunk_of(c)]
+        to_peers(Q_ROW, nat2, put_into(sendb.at[COT, c]))
+
+    fetches[2].wait()
+    first_cot(0)
+    pl.semaphore_wait(barrier, PEERS - 1 + SAMP - 1)
+    send(COT, 0)
     fetches[0].wait()
     for b in range(OWN):
         rt[0, b] = right[0, b].T
     fetches[1].wait()
     first(0)
-
-    pl.semaphore_wait(barrier, PEERS - 1 + SAMP - 1)
-
     send(U1, 0)
 
     pick = onehot((lax.broadcasted_iota(jnp.int32, (BLOCK, 128), 0) & 3) == (lax.broadcasted_iota(jnp.int32, (BLOCK, 128), 1) & 3)).astype(F32)
     lane = lax.broadcasted_iota(jnp.int32, (PEERS, 128), 1)
     owner = lax.broadcasted_iota(jnp.int32, (PEERS, BLOCK), 0)
     unit = lax.broadcasted_iota(jnp.int32, (PEERS, BLOCK), 1)
+    fetches[6].wait()
     message = jnp.zeros((PEERS, 128), F32)
     for r in range(ROWS):
         row = mixing[r // 8, (r // 4) % 2, r % 4 : r % 4 + 1, :]
@@ -186,11 +194,8 @@
     qmat[Q_ROW_T] = onehot(i0 == row_of(i1))
     qmat[Q_COL] = onehot(i1 == col_of(i0))
     qmat[Q_COL_T] = onehot(i0 == col_of(i1))
-    fetches[2].wait()
-    for c in range(CHUNKS):
-        for b in range(OWN):
-            nat[b] = cot[b, :, chunk_of(c)]
-        to_peers(Q_ROW, nat, put_into(sendb.at[COT, c]))
+    for c in range(1, CHUNKS):
+        first_cot(c)
     for n in (3, 4, 5):
         fetches[n].wait()
     for b in range(OWN):
@@ -280,10 +285,11 @@
             nat[j] = mm(lt[0, j], vn[0, c, j]).astype(BF16)
         to_peers(Q_COL, nat, put_into(sendb.at[T1, c]))
         send(T1, c)
+        return carry
+
+    lax.fori_loop(0, CHUNKS, col1, 0)
+    for c in range(1, CHUNKS):
         send(COT, c)
-        return carry
-
-    lax.fori_loop(0, CHUNKS, col1, 0)
 
     def row2(c, carry):
         wait_recv(T1, c)
@@ -356,13 +362,13 @@
     send(DU1, 0)
     col1_grad(0)
     mix_gradient(0, U1, 0)
+    col1_back(1)
+    send(DU1, 1, 1, SPLIT)
+    col1_grad(1)
+    scatter(GL1)
+    mix_gradient(0, U1, 1)
     gather(GR2)
     store(GL2)
-    col1_back(1)
-    col1_grad(1)
-    scatter(GL1)
-    send(DU1, 1, 1, SPLIT)
-    mix_gradient(0, U1, 1)
     gms[...] = gmacc[...].reshape(PEERS, 1, 128)
 
     def send_gm(k, carry):
@@ -452,12 +458,23 @@
     wait_all(fgradb, o_sem.at[5])
 
 
-def finish(out_in, fgrad_in, gright_in, gleft_in, gmix_in, out, fgrad, gright, gleft, gmix):
-    out[...] = out_in[...]
-    fgrad[...] = fgrad_in[...]
-    gright[...] = gright_in[...].astype(F32)
-    gleft[...] = gleft_in[...].astype(F32)
-    gmix[...] = gmix_in[...]
+def finish(out_in, fgrad_in, gright_in, gleft_in, gmix_in, out, fgrad, gright, gleft, gmix, wide, sem):
+    whole = [
+        pltpu.make_async_copy(src, dst, sem.at[0, n])
+        for n, (src, dst) in enumerate(((out_in, out), (fgrad_in, fgrad), (gmix_in, gmix)))
+    ]
+    for copy in whole:
+        copy.start()
+    pieces = []
+    for n, (src, dst) in enumerate(((gright_in, gright), (gleft_in, gleft))):
+        for layer in range(LAYERS):
+            for b in range(OWN):
+                wide[n, layer, b] = src[layer, b].astype(F32)
+                copy = pltpu.make_async_copy(wide.at[n, layer, b], dst.at[layer, b], sem.at[1 + n, OWN * layer + b])
+                copy.start()
+                pieces.append(copy)
+    for copy in whole + pieces:
+        copy.wait()
 
 
 def local(features, cotangent, right_factor, left_factor, mixing):
@@ -472,13 +489,14 @@
     output, fgrad, gright, gleft, gmix = pl.pallas_call(
         kernel,
         out_shape=(acts, acts, grads, grads, jax.ShapeDtypeStruct((LAYERS, 2, OWN, BLOCK), F32)),
-        in_specs=[hbm] * 4 + [vmem],
+        in_specs=[pl.BlockSpec(memory_space=pltpu.HBM)] * 5,
         out_specs=(hbm, hbm, hbm, hbm, vmem),
         scratch_shapes=[
             pltpu.VMEM((OWN, BLOCK, width), BF16),
             pltpu.VMEM((OWN, BLOCK, width), BF16),
             pltpu.VMEM((LAYERS, OWN, BLOCK, BLOCK), BF16),
             pltpu.VMEM((LAYERS, OWN, BLOCK, BLOCK), F32),
+            pltpu.VMEM((LAYERS, 2, OWN, BLOCK), F32),
             pltpu.VMEM((8, CHUNKS, PEERS, ROWS, samples), BF16),
             pltpu.VMEM((8, CHUNKS, PEERS, ROWS, samples), BF16),
             pltpu.VMEM((4, BLOCK, BLOCK), BF16),
@@ -515,40 +533,36 @@
             pltpu.SemaphoreType.DMA((4,)),
             pltpu.SemaphoreType.DMA((4,)),
             pltpu.SemaphoreType.DMA((6,)),
-            pltpu.SemaphoreType.DMA((6,)),
+            pltpu.SemaphoreType.DMA((7,)),
         ],
         compiler_params=pltpu.CompilerParams(
-            collective_id=0, has_side_effects=True, vmem_limit_bytes=58 * 1024 * 1024
+            collective_id=0, has_side_effects=True, vmem_limit_bytes=48 * 1024 * 1024
         ),
     )(
-        features.reshape(OWN, BLOCK, width),
-        cotangent.reshape(OWN, BLOCK, width),
-        right_factor,
-        left_factor,
-        mixing,
+        *(
+            pltpu.with_memory_space_constraint(value, pltpu.HBM)
+            for value in (
+                features.reshape(OWN, BLOCK, width),
+                cotangent.reshape(OWN, BLOCK, width),
+                right_factor,
+                left_factor,
+                mixing,
+            )
+        )
     )
-    rows = OWN * BLOCK
-    step = rows // FINAL
-    blocks = LAYERS * OWN // FINAL
-    wide = pl.BlockSpec((step, width), lambda i: (i, 0))
-    block = pl.BlockSpec((blocks, BLOCK, BLOCK), lambda i: (i, 0, 0))
-    whole = pl.BlockSpec((LAYERS, 2, OWN, BLOCK), lambda i: (0, 0, 0, 0))
-    flat = (LAYERS * OWN, BLOCK, BLOCK)
+    wide = jax.ShapeDtypeStruct((LAYERS, OWN, BLOCK, BLOCK), F32)
     output, fgrad, gright, gleft, gmix = pl.pallas_call(
         finish,
-        grid=(FINAL,),
-        out_shape=(
-            jax.ShapeDtypeStruct((rows, width), BF16),
-            jax.ShapeDtypeStruct((rows, width), BF16),
-            jax.ShapeDtypeStruct(flat, F32),
-            jax.ShapeDtypeStruct(flat, F32),
-            jax.ShapeDtypeStruct((LAYERS, 2, OWN, BLOCK), F32),
-        ),
-        in_specs=[wide, wide, block, block, whole],
-        out_specs=(wide, wide, block, block, whole),
-    )(output.reshape(rows, width), fgrad.reshape(rows, width), gright.reshape(flat), gleft.reshape(flat), gmix)
-    shape = (LAYERS, OWN, BLOCK, BLOCK)
-    return output, fgrad, gright.reshape(shape), gleft.reshape(shape), gmix
+        out_shape=(acts, acts, wide, wide, jax.ShapeDtypeStruct((LAYERS, 2, OWN, BLOCK), F32)),
+        in_specs=[hbm, hbm, vmem, vmem, hbm],
+        out_specs=[hbm] * 5,
+        scratch_shapes=[
+            pltpu.VMEM((2, LAYERS, OWN, BLOCK, BLOCK), F32),
+            pltpu.SemaphoreType.DMA((3, LAYERS * OWN)),
+        ],
+        compiler_params=pltpu.CompilerParams(vmem_limit_bytes=12 * 1024 * 1024),
+    )(output, fgrad, gright, gleft, gmix)
+    return output.reshape(OWN * BLOCK, width), fgrad.reshape(OWN * BLOCK, width), gright, gleft, gmix
 
 
 def solution(mesh):

time: 211 us -> 206 us (0.976)
  Pallas kernels: 210 us -> 205 us
    pallas_call x1, Pallas kernels: 5.25 us -> 2.85 us  [local(): pl.pallas_call(finish, out_shape=(acts, acts, wide, wide, jax.ShapeDtypeS...]
where the time goes in v4:
time: 206 us
  Pallas kernels  205 us (100%)
    pallas_call x1, Pallas kernels, local(): pl.pallas_call(kernel, out_shape=(acts, acts, grads, grads, jax.ShapeDtyp...  203 us

profile of v4, /device:TPU:1, one launch (start us, length us, event | category | flops | bytes accessed | tf_op | source)
XLA Modules:
  0.0 206.2 jit_solution(3971195063900957774)
XLA Ops:
  0.6 202.6 %shard_map.92 = (bf16[4,256,512]{2,1,0:T(8,128)(2,1)S(1)}, bf16[4,256,512]{2,1,0:T(8,128)(2,1)S(1)}, bf16[2,4,256,256]{3,2,1,0:T(8,128)(2,1)S(1)}, bf16[2,4,256,...) custom-call(bf16[4,256,512]{2,1,0:T(8,128)(2,1)} %bitcast.4, bf16[4,256,512]{2,1,0:T(8,128)(2,1)} %bitcast.5, ...), custom_call_target="tpu_custom_call" | custom-call | tf_op jit(solution)/shard_map/pallas_call | solution.py:489
  203.2 2.9 %shard_map.93 = (bf16[4,256,512]{2,1,0:T(8,128)(2,1)}, bf16[4,256,512]{2,1,0:T(8,128)(2,1)}, f32[2,4,256,256]{3,2,1,0:T(8,128)}, f32[2,4,256,256]{3,2,1,0:T(8,128)}, f32[2,2,4,256]{3,2,1,0:T(4,128)}) custom-call(bf16[4,256,512]{2,1,0:T(8,128)(2,1)S(1)} %get-tuple-element.15.out_in, bf16[4,256,512]{2,1,0:T(8,128)(2,1)S(1)} %get-tuple-element.16.fgrad_in, ...), custom_call_target="tpu_custom_call" | custom-call | tf_op jit(solution)/shard_map/pallas_call | solution.py:554

commit v5 on v4

--- a/solution.py
+++ b/solution.py
@@ -16,9 +16,8 @@
 GPEERS = PEERS // GROUPS
 SAMP = 4
 CHUNKS = 2
-EARLY = 40
-LATE = 17
-SPLIT = 33
+CUT_A = 50
+CUT_B = 20
 MESH = pl.DeviceIdType.MESH
 F32 = jnp.float32
 BF16 = jnp.bfloat16
@@ -309,7 +308,7 @@
         s = jax.nn.sigmoid(t)
         return (g * s * (1.0 + t * (1.0 - s))).astype(BF16)
 
-    def col2(c, carry):
+    def col2(c):
         wait_recv(COT, c)
         from_peers(Q_COL_T, recvb.at[COT, c], nat2)
         wait_recv(U2, c)
@@ -320,17 +319,17 @@
             e = slope(nat2[j].astype(F32), t.astype(F32))
             gacc[GL2, j] += mm_t(vn[1, c, j], e)
             nat2[j] = mm(lb[1, j], e).astype(BF16)
+        if c == CHUNKS - 1:
+            scatter(GL2)
         mix_backward(1, DU2, c)
         send(DU2, c)
         to_peers(Q_COL, nat, put_into(sendb.at[T2, c]))
         mix_gradient(1, U2, c)
-        return carry
-
-    lax.fori_loop(0, CHUNKS, col2, 0)
-    scatter(GL2)
-    send(T2, 0, 1, EARLY)
-
-    def row1(c, carry):
+
+    for c in range(CHUNKS):
+        col2(c)
+
+    def row1(c):
         wait_recv(DU2, c)
         from_peers(Q_ROW_T, recvb.at[DU2, c], nat)
         for b in range(OWN):
@@ -338,14 +337,19 @@
             g1[c, b] = g
             nat2[b] = slope(g.astype(F32), t1[c, b].astype(F32))
         to_peers(Q_ROW, nat2, put_into(sendb.at[E1, c]))
-        send(E1, c)
+
+    def row1_grad(c):
         for b in range(OWN):
             gacc[GR2, b] += mm_t(h1[c, b], nat[b])
-        return carry
-
-    lax.fori_loop(0, CHUNKS, row1, 0)
+
+    row1(0)
+    send(E1, 0)
+    row1_grad(0)
     gather(GL2)
+    row1(1)
+    row1_grad(1)
     scatter(GR2)
+    send(E1, 1)
 
     def col1_back(c):
         wait_recv(E1, c)
@@ -362,12 +366,12 @@
     send(DU1, 0)
     col1_grad(0)
     mix_gradient(0, U1, 0)
+    gather(GR2)
     col1_back(1)
-    send(DU1, 1, 1, SPLIT)
     col1_grad(1)
     scatter(GL1)
+    send(DU1, 1)
     mix_gradient(0, U1, 1)
-    gather(GR2)
     store(GL2)
     gms[...] = gmacc[...].reshape(PEERS, 1, 128)
 
@@ -381,9 +385,9 @@
 
     lax.fori_loop(1, PEERS, send_gm, 0)
     gm1[pl.ds(me, 1)] = gms[pl.ds(me, 1)]
+    store(GR2)
     gather(GL1)
-    send(DU1, 1, SPLIT, PEERS)
-    store(GR2)
+    send(T2, 0, 1, CUT_A)
 
     dun = h1d
 
@@ -404,9 +408,8 @@
             src_ref=gm1, dst_ref=gmy.at[y], send_sem=r_send.at[4], recv_sem=r_recv.at[4],
             device_id={"samp": to}, device_id_type=MESH,
         ).start()
-    if EARLY < PEERS:
-        send(T2, 0, EARLY, PEERS)
-    send(T2, 1, 1, LATE)
+    send(T2, 0, CUT_A, PEERS)
+    send(T2, 1, 1, CUT_B)
 
     def row0_grad(c, carry):
         for b in range(OWN):
@@ -417,7 +420,7 @@
     pltpu.make_async_copy(fgradb, fgrad_hbm, o_sem.at[5]).start()
     store(GL1)
     gather(GR1)
-    send(T2, 1, LATE, PEERS)
+    send(T2, 1, CUT_B, PEERS)
     wait_all(gmy.at[pl.ds(0, SAMP - 1)], r_recv.at[4])
     total = (gmy[0] + gmy[1] + gmy[2] + gmy[3]).reshape(PEERS, 128)
     spread_back = onehot(

time: 206 us -> 199 us (0.966)
  Pallas kernels: 205 us -> 199 us
    pallas_call x1, Pallas kernels: 203 us -> 196 us  [local(): pl.pallas_call(kernel, out_shape=(acts, acts, grads, grads, jax.ShapeDtyp...]
where the time goes in v5:
time: 199 us
  Pallas kernels  199 us (100%)
    pallas_call x1, Pallas kernels, local(): pl.pallas_call(kernel, out_shape=(acts, acts, grads, grads, jax.ShapeDtyp...  196 us

profile of v5, /device:TPU:1, one launch (start us, length us, event | category | flops | bytes accessed | tf_op | source)
XLA Modules:
  0.0 199.3 jit_solution(12760680900959933991)
XLA Ops:
  0.6 195.7 %shard_map.92 = (bf16[4,256,512]{2,1,0:T(8,128)(2,1)S(1)}, bf16[4,256,512]{2,1,0:T(8,128)(2,1)S(1)}, bf16[2,4,256,256]{3,2,1,0:T(8,128)(2,1)S(1)}, bf16[2,4,256,...) custom-call(bf16[4,256,512]{2,1,0:T(8,128)(2,1)} %bitcast.4, bf16[4,256,512]{2,1,0:T(8,128)(2,1)} %bitcast.5, ...), custom_call_target="tpu_custom_call" | custom-call | tf_op jit(solution)/shard_map/pallas_call | solution.py:492
  196.3 2.9 %shard_map.93 = (bf16[4,256,512]{2,1,0:T(8,128)(2,1)}, bf16[4,256,512]{2,1,0:T(8,128)(2,1)}, f32[2,4,256,256]{3,2,1,0:T(8,128)}, f32[2,4,256,256]{3,2,1,0:T(8,128)}, f32[2,2,4,256]{3,2,1,0:T(4,128)}) custom-call(bf16[4,256,512]{2,1,0:T(8,128)(2,1)S(1)} %get-tuple-element.15.out_in, bf16[4,256,512]{2,1,0:T(8,128)(2,1)S(1)} %get-tuple-element.16.fgrad_in, ...), custom_call_target="tpu_custom_call" | custom-call | tf_op jit(solution)/shard_map/pallas_call | solution.py:557

commit v6 on v5

--- a/solution.py
+++ b/solution.py
@@ -16,8 +16,7 @@
 GPEERS = PEERS // GROUPS
 SAMP = 4
 CHUNKS = 2
-CUT_A = 50
-CUT_B = 20
+TAIL_CUT = 33
 MESH = pl.DeviceIdType.MESH
 F32 = jnp.float32
 BF16 = jnp.bfloat16
@@ -387,7 +386,7 @@
     gm1[pl.ds(me, 1)] = gms[pl.ds(me, 1)]
     store(GR2)
     gather(GL1)
-    send(T2, 0, 1, CUT_A)
+    send(T2, 0)
 
     dun = h1d
 
@@ -408,8 +407,7 @@
             src_ref=gm1, dst_ref=gmy.at[y], send_sem=r_send.at[4], recv_sem=r_recv.at[4],
             device_id={"samp": to}, device_id_type=MESH,
         ).start()
-    send(T2, 0, CUT_A, PEERS)
-    send(T2, 1, 1, CUT_B)
+    send(T2, 1, 1, TAIL_CUT)
 
     def row0_grad(c, carry):
         for b in range(OWN):
@@ -420,7 +418,7 @@
     pltpu.make_async_copy(fgradb, fgrad_hbm, o_sem.at[5]).start()
     store(GL1)
     gather(GR1)
-    send(T2, 1, CUT_B, PEERS)
+    send(T2, 1, TAIL_CUT, PEERS)
     wait_all(gmy.at[pl.ds(0, SAMP - 1)], r_recv.at[4])
     total = (gmy[0] + gmy[1] + gmy[2] + gmy[3]).reshape(PEERS, 128)
     spread_back = onehot(
@@ -443,9 +441,10 @@
             outb[b, :, chunk_of(c)] = (h1[c, b].astype(F32) + t * jax.nn.sigmoid(t)).astype(BF16)
         return carry
 
-    lax.fori_loop(0, CHUNKS, final_output, 0)
+    final_output(0, 0)
+    store(GR1)
+    final_output(1, 0)
     pltpu.make_async_copy(outb, out_hbm, o_sem.at[4]).start()
-    store(GR1)
 
     for a in range(8):
         for c in range(CHUNKS):

time: 199 us -> 199 us (level)
  no operation moved by 1% of the time
where the time goes in v6:
time: 199 us
  Pallas kernels  198 us (99%)
    pallas_call x1, Pallas kernels, local(): pl.pallas_call(kernel, out_shape=(acts, acts, grads, grads, jax.ShapeDtyp...  195 us

profile of v6, /device:TPU:1, one launch (start us, length us, event | category | flops | bytes accessed | tf_op | source)
XLA Modules:
  0.0 199.0 jit_solution(6057832637000456298)
XLA Ops:
  0.6 195.3 %shard_map.92 = (bf16[4,256,512]{2,1,0:T(8,128)(2,1)S(1)}, bf16[4,256,512]{2,1,0:T(8,128)(2,1)S(1)}, bf16[2,4,256,256]{3,2,1,0:T(8,128)(2,1)S(1)}, bf16[2,4,256,...) custom-call(bf16[4,256,512]{2,1,0:T(8,128)(2,1)} %bitcast.4, bf16[4,256,512]{2,1,0:T(8,128)(2,1)} %bitcast.5, ...), custom_call_target="tpu_custom_call" | custom-call | tf_op jit(solution)/shard_map/pallas_call | solution.py:491
  196.0 2.9 %shard_map.93 = (bf16[4,256,512]{2,1,0:T(8,128)(2,1)}, bf16[4,256,512]{2,1,0:T(8,128)(2,1)}, f32[2,4,256,256]{3,2,1,0:T(8,128)}, f32[2,4,256,256]{3,2,1,0:T(8,128)}, f32[2,2,4,256]{3,2,1,0:T(4,128)}) custom-call(bf16[4,256,512]{2,1,0:T(8,128)(2,1)S(1)} %get-tuple-element.15.out_in, bf16[4,256,512]{2,1,0:T(8,128)(2,1)S(1)} %get-tuple-element.16.fgrad_in, ...), custom_call_target="tpu_custom_call" | custom-call | tf_op jit(solution)/shard_map/pallas_call | solution.py:556

commit v7 on v6

--- a/solution.py
+++ b/solution.py
@@ -397,8 +397,19 @@
             gacc[GR1, b] += mm_t(feat[b, :, chunk_of(c)], dun[c, b])
         return carry
 
-    lax.fori_loop(0, CHUNKS, row0, 0)
-    scatter(GR1)
+    row0(0, 0)
+    last = CHUNKS - 1
+    wait_recv(DU1, last)
+    from_peers(Q_ROW_T, recvb.at[DU1, last], dun.at[last])
+    for d in range(1, SAMP + 1):
+        to = lax.rem(y + d, SAMP)
+        gacc[GR1, to] += mm_t(feat[to, :, chunk_of(last)], dun[last, to])
+        if d < SAMP:
+            gsend[GR1, to] = gacc[GR1, to].astype(BF16)
+            pltpu.make_async_remote_copy(
+                src_ref=gsend.at[GR1, to], dst_ref=rsr.at[GR1, y], send_sem=r_send.at[GR1], recv_sem=r_recv.at[GR1],
+                device_id={"samp": to}, device_id_type=MESH,
+            ).start()
     wait_all(gm1.at[pl.ds(0, PEERS - 1)], m_recv.at[1])
     gmy[pl.ds(y, 1)] = gm1[...].reshape(1, PEERS, 1, 128)
     for d in range(1, SAMP):
@@ -452,7 +463,7 @@
     wait_all(mixs.at[pl.ds(0, PEERS - 1)], m_send.at[0])
     wait_all(gms.at[pl.ds(0, PEERS - 1)], m_send.at[1])
     for a in range(4):
-        wait_all(gsend.at[a, pl.ds(0, SAMP - 1)], r_send.at[a])
+        wait_all(rsr.at[a, pl.ds(0, SAMP - 1)], r_send.at[a])
         wait_all(ag.at[a, pl.ds(0, SAMP - 1)], g_send.at[a])
         wait_all(ag.at[a], o_sem.at[a])
     wait_all(gmy.at[pl.ds(0, SAMP - 1)], r_send.at[4])

time: 199 us -> 199 us (level)
  no operation moved by 1% of the time
where the time goes in v7:
time: 199 us
  Pallas kernels  198 us (99%)
    pallas_call x1, Pallas kernels, local(): pl.pallas_call(kernel, out_shape=(acts, acts, grads, grads, jax.ShapeDtyp...  195 us

profile of v7, /device:TPU:1, one launch (start us, length us, event | category | flops | bytes accessed | tf_op | source)
XLA Modules:
  0.0 199.0 jit_solution(8714573744612572918)
XLA Ops:
  0.6 195.3 %shard_map.92 = (bf16[4,256,512]{2,1,0:T(8,128)(2,1)S(1)}, bf16[4,256,512]{2,1,0:T(8,128)(2,1)S(1)}, bf16[2,4,256,256]{3,2,1,0:T(8,128)(2,1)S(1)}, bf16[2,4,256,...) custom-call(bf16[4,256,512]{2,1,0:T(8,128)(2,1)} %bitcast.4, bf16[4,256,512]{2,1,0:T(8,128)(2,1)} %bitcast.5, ...), custom_call_target="tpu_custom_call" | custom-call | tf_op jit(solution)/shard_map/pallas_call | solution.py:502
  196.0 2.9 %shard_map.93 = (bf16[4,256,512]{2,1,0:T(8,128)(2,1)}, bf16[4,256,512]{2,1,0:T(8,128)(2,1)}, f32[2,4,256,256]{3,2,1,0:T(8,128)}, f32[2,4,256,256]{3,2,1,0:T(8,128)}, f32[2,2,4,256]{3,2,1,0:T(4,128)}) custom-call(bf16[4,256,512]{2,1,0:T(8,128)(2,1)S(1)} %get-tuple-element.15.out_in, bf16[4,256,512]{2,1,0:T(8,128)(2,1)S(1)} %get-tuple-element.16.fgrad_in, ...), custom_call_target="tpu_custom_call" | custom-call | tf_op jit(solution)/shard_map/pallas_call | solution.py:567
